TPU v7x, 32 devices: a whole 2x2x4 slice. The times are simulated.
32 devices in a mesh: dom: 32 (over z, y, x, core).
Axes of the slice: x: 2, y: 2, z: 4, core: 2. Of those that a mesh axis runs over, the one named last changes fastest.
Arguments:
- features: bfloat16 [64, 262144], P(None, 'dom'), may hold values from -6 to 6
- cheb_weight: bfloat16 [4, 64, 64], replicated, may hold values from -0.375 to 0.375
- lap_tiles: bfloat16 [2048, 3, 128, 128], P('dom'), may hold values from -0.25 to 0.25
- col_index: int32 [2048, 3], P('dom'), may hold values from 0 to 63
- cross_tiles: bfloat16 [32, 5, 2, 128, 128], P('dom'), may hold values from -0.25 to 0.25
- send_index: int32 [32, 5, 2], P('dom'), may hold values from 0 to 63
- row_index: int32 [32, 5, 2], P('dom'), may hold values from 0 to 63
- pair_on: int32 [32, 5], P('dom'), may hold values 0 or 1
- blk_live: int32 [32], P('dom'), may hold values from 1 to 64, 1536 in all
- cotangent: bfloat16 [64, 262144], P(None, 'dom'), may hold values from -6 to 6
Outputs:
- conv_out: bfloat16 [64, 262144], P(None, 'dom')
- grad_x: bfloat16 [64, 262144], P(None, 'dom')
- grad_w: float32 [4, 64, 64], replicated
Inputs may be any that keep to these rules, and one draw needn't show every extreme that they name: `blk_live`: the counts sum to 1536 and the largest is exactly 64.
All inputs are finite; a program needn't handle non-finite values. No bound on the sum of `pair_on` or of `blk_live` on one device may be relied on, other than what follows from the above.
Results may differ from a plain program's by a relative error of at most 0.0059.
Values may be sent and summed in bfloat16 or wider, within the bound.
No kernel may reach another device: no remote copies, remote signals or barrier semaphores. Data moves between devices by JAX's collectives and lax.ppermute only.
A program may use at most 128 MiB of HBM per device.

v0:
```python
import functools

import jax
import jax.numpy as jnp
from jax import lax
from jax.experimental import pallas as pl
from jax.experimental.pallas import tpu as pltpu
from jax.sharding import PartitionSpec as P


F32 = jnp.float32
BF16 = jnp.bfloat16
SUB = 8
LANES = 128
ROWS_FIRST = 8
ROWS_PART = 16
ROWS = 32

VMEM = pl.BlockSpec(memory_space=pltpu.VMEM)
SMEM = pl.BlockSpec(memory_space=pltpu.SMEM)
HBM = pl.BlockSpec(memory_space=pltpu.HBM)
TOKEN = jax.ShapeDtypeStruct((SUB, LANES), F32)


def shape(dims, dtype):
    return jax.ShapeDtypeStruct(dims, dtype)


def nn(a, b):
    return lax.dot_general(a, b, (((1,), (0,)), ((), ())), preferred_element_type=F32)


class Sizes:
    def __init__(self, features, lap_tiles, cross_tiles):
        self.chan = features.shape[0]
        self.blocks, self.nz, self.blk = lap_tiles.shape[:3]
        self.rounds, self.hb = cross_tiles.shape[1:3]
        self.pairs = self.rounds * self.hb
        self.rows = 0
        self.sends = self.pairs
        self.first_row = 2 * self.pairs
        self.first_send = 3 * self.pairs
        self.flags = 4 * self.pairs
        self.live = self.flags + self.rounds
        self.meta = self.live + 1
        self.half = self.hb * self.chan
        self.field = shape((self.blocks, self.chan, self.blk), BF16)
        self.picked = shape((self.pairs, self.chan, self.blk), F32)
        self.pay = shape((2 * self.half, self.blk), BF16)

    def couplings(self):
        return [(r, h, r * self.hb + h) for r in range(self.rounds) for h in range(self.hb)]

    def forward_part(self, h):
        return pl.ds(h * self.chan, self.chan)

    def adjoint_part(self, h):
        return pl.ds(self.half + h * self.chan, self.chan)


def call(kernel, in_specs, out_specs, out_shape, scratch, flops, moved, limit, aliases=None):
    return pl.pallas_call(
        kernel,
        in_specs=in_specs,
        out_specs=out_specs,
        out_shape=out_shape,
        scratch_shapes=scratch,
        input_output_aliases=aliases or {},
        compiler_params=pltpu.CompilerParams(vmem_limit_bytes=limit << 20),
        cost_estimate=pl.CostEstimate(flops=flops, bytes_accessed=moved, transcendentals=0),
    )


def fill_pays(sz, meta, tnew, snew, cross, pays):
    for r, h, j in sz.couplings():
        pays[r][sz.forward_part(h), :] = tnew[meta[sz.sends + j]]
        term = nn(snew[meta[sz.rows + j]], cross[j])
        factor = meta[sz.flags + r].astype(F32)
        pays[r][sz.adjoint_part(h), :] = (factor * term).astype(BF16)


def pack_kernel(sz, *refs):
    x4, u4, coupling, send, row, pair, live_s, col = refs[:8]
    xb, ub, cross, across, meta, col_out = refs[8:14]
    pays = refs[14 : 14 + sz.rounds]
    send_s, row_s, pair_s, sem_x, sem_u, sem_t, sem_i = refs[14 + sz.rounds :]
    small = [
        pltpu.make_async_copy(send, send_s, sem_i.at[0]),
        pltpu.make_async_copy(row, row_s, sem_i.at[1]),
        pltpu.make_async_copy(pair, pair_s, sem_i.at[2]),
    ]
    tiles = pltpu.make_async_copy(coupling, cross, sem_t)
    copies = []
    for t in range(sz.chan // SUB):
        part = pl.ds(t * SUB, SUB)
        copies.append(pltpu.make_async_copy(x4.at[t], xb.at[:, part, :], sem_x.at[t]))
        copies.append(pltpu.make_async_copy(u4.at[t], ub.at[:, part, :], sem_u.at[t]))
    copies.append(pltpu.make_async_copy(col, col_out, sem_i.at[3]))
    for copy in small + [tiles] + copies:
        copy.start()
    for copy in small:
        copy.wait()
    count = live_s[0]
    rows = [lax.rem(row_s[0, h, r], count) for r, h, _ in sz.couplings()]
    sends = [lax.rem(send_s[0, h, r], count) for r, h, _ in sz.couplings()]
    for values, spot, first in (
        (rows, sz.rows, sz.first_row),
        (sends, sz.sends, sz.first_send),
    ):
        for j, value in enumerate(values):
            earliest = jnp.int32(j)
            for q in reversed(range(j)):
                earliest = jnp.where(values[q] == value, q, earliest)
            meta[spot + j] = value
            meta[first + j] = earliest
    for r in range(sz.rounds):
        meta[sz.flags + r] = pair_s[0, r]
    meta[sz.live] = count
    tiles.wait()
    for j in range(sz.pairs):
        across[j] = cross[j].T
    for copy in copies:
        copy.wait()

    def clear(i, carry):
        xb[i] = jnp.zeros(xb.shape[1:], BF16)
        ub[i] = jnp.zeros(ub.shape[1:], BF16)
        return carry

    lax.fori_loop(count, sz.blocks, clear, 0)
    fill_pays(sz, meta, xb, ub, cross, pays)


def keep(array):
    return pltpu.with_memory_space_constraint(array, pltpu.HBM)


def pack(sz, *args):
    args = [array if array.size == 1 else keep(array) for array in args]
    _, _, _, send, row, pair, _, col = args
    groups = sz.chan // SUB
    cross = shape((sz.pairs, sz.blk, sz.blk), BF16)
    table = pltpu.SMEM((sz.meta,), jnp.int32)
    return call(
        functools.partial(pack_kernel, sz),
        [HBM] * 6 + [SMEM, HBM],
        [VMEM] * 4 + [SMEM, SMEM] + [VMEM] * sz.rounds,
        [sz.field, sz.field, cross, cross, table, pltpu.SMEM(col.shape, jnp.int32)]
        + [sz.pay] * sz.rounds,
        [
            pltpu.SMEM(send.shape, jnp.int32),
            pltpu.SMEM(row.shape, jnp.int32),
            pltpu.SMEM(pair.shape, jnp.int32),
            pltpu.SemaphoreType.DMA((groups,)),
            pltpu.SemaphoreType.DMA((groups,)),
            pltpu.SemaphoreType.DMA,
            pltpu.SemaphoreType.DMA((4,)),
        ],
        1000,
        4 << 20,
        8,
    )(*args)


def big_steps(count):
    return (count + ROWS - 1) // ROWS


def part_steps(count):
    return (count + ROWS_PART - 1) // ROWS_PART


def clear_sums(sz, summed):
    def clear(i, carry):
        summed[i] = jnp.zeros(summed.shape[1:], F32)
        return carry

    lax.fori_loop(0, sz.blocks, clear, 0, unroll=4)


def scatter_terms(sz, summed, cols, terms):
    for m in range(sz.nz):
        summed[cols[m]] = summed[cols[m]] + terms[:, m * sz.blk : (m + 1) * sz.blk]


def finish_local(sz, meta, held, adjoint, tnew, snew, psel, qsel):
    count = meta[sz.live]

    def finish(g, carry):
        for u in range(ROWS):
            i = g * ROWS + u
            snew[i] = adjoint(i).astype(BF16)
        return carry

    lax.fori_loop(0, big_steps(count), finish, 0)

    def dead(i, carry):
        tnew[i] = jnp.zeros(tnew.shape[1:], BF16)
        snew[i] = jnp.zeros(snew.shape[1:], BF16)
        return carry

    lax.fori_loop(count, sz.blocks, dead, 0)
    for j in range(sz.pairs):
        psel[j] = held[meta[sz.rows + j]]
        qsel[j] = adjoint(meta[sz.sends + j])


def first_kernel(sz, *refs):
    meta, col, tiles_hbm, t0, s0 = refs[:5]
    tnew, snew, psel, qsel, tiles, turned, gram, held, summed, sem = refs[5:]
    count = meta[sz.live]
    steps = big_steps(count)
    loads = steps * (ROWS // ROWS_FIRST)

    def fetch(g):
        part = pl.ds(g * ROWS_FIRST, ROWS_FIRST)
        return pltpu.make_async_copy(tiles_hbm.at[part], tiles.at[part], sem.at[g])

    def start(g, carry):
        fetch(g).start()
        return carry

    lax.fori_loop(0, loads, start, 0)
    clear_sums(sz, summed)

    def products(g, total):
        spots = [g * ROWS + u for u in range(ROWS)]
        left = jnp.concatenate([t0[i] for i in spots], axis=1)
        return total + nn(left, jnp.concatenate([s0[i].T for i in spots], axis=0))

    gram[...] = lax.fori_loop(0, steps, products, jnp.zeros(gram.shape, F32))

    def block_row(i):
        cols = [col[m, i] for m in range(sz.nz)]
        parts = [tiles[i, m] for m in range(sz.nz)]
        flipped = [part.T for part in parts]
        for m in range(sz.nz):
            turned[i, pl.ds(m * sz.blk, sz.blk), :] = flipped[m]
        gathered = jnp.concatenate([t0[c] for c in cols], axis=1)
        forward = nn(gathered, jnp.concatenate(flipped, axis=0))
        held[i] = forward
        tnew[i] = forward.astype(BF16)
        scatter_terms(sz, summed, cols, nn(s0[i], jnp.concatenate(parts, axis=1)))

    def stepper(rows):
        def step(g, carry):
            for part in range(rows // ROWS_FIRST):
                fetch(g * (rows // ROWS_FIRST) + part).wait()
            for u in range(rows):
                block_row(g * rows + u)
            return carry

        return step

    short = ROWS // ROWS_PART
    lax.fori_loop(0, short, stepper(ROWS_PART), 0)
    lax.fori_loop(1, steps, stepper(ROWS), 0)
    finish_local(sz, meta, held, lambda i: summed[i], tnew, snew, psel, qsel)


def first_products(sz, meta, col, tiles, t0, s0):
    turned = shape((sz.blocks, sz.nz * sz.blk, sz.blk), BF16)
    return call(
        functools.partial(first_kernel, sz),
        [SMEM, SMEM, HBM, VMEM, VMEM],
        [VMEM] * 7,
        [sz.field, sz.field, sz.picked, sz.picked, shape(tiles.shape, BF16), turned]
        + [shape((sz.chan, sz.chan), F32)],
        [pltpu.VMEM((sz.blocks, sz.chan, sz.blk), F32)] * 2
        + [pltpu.SemaphoreType.DMA((sz.blocks // ROWS_FIRST,))],
        4 * sz.blocks * sz.nz * sz.chan * sz.blk * sz.blk,
        12 << 20,
        24,
    )(meta, col, keep(tiles), t0, s0)


def row_products(sz, col, low, high, rows, arrays, tnew, held, summed):
    tiles, turned, tcur, scur, tprev = arrays

    def block_row(i):
        cols = [col[m, i] for m in range(sz.nz)]
        gathered = jnp.concatenate([tcur[c] for c in cols], axis=1)
        forward = 2.0 * nn(gathered, turned[i]) - tprev[i].astype(F32)
        held[i] = forward
        tnew[i] = forward.astype(BF16)
        wide = jnp.concatenate([tiles[i, m] for m in range(sz.nz)], axis=1)
        scatter_terms(sz, summed, cols, nn(scur[i], wide))

    def step(g, carry):
        for u in range(rows):
            block_row(g * rows + u)
        return carry

    lax.fori_loop(low, high, step, 0)


def local_kernel(sz, *refs):
    meta, col, tiles, turned, tcur, scur, tprev, sprev = refs[:8]
    tnew, snew, psel, qsel, gram, held, summed = refs[8:]
    clear_sums(sz, summed)
    steps = big_steps(meta[sz.live])
    arrays = (tiles, turned, tcur, scur, tprev)
    row_products(sz, col, 0, steps, ROWS, arrays, tnew, held, summed)

    def adjoint(i):
        return 2.0 * summed[i] - sprev[i].astype(F32)

    finish_local(sz, meta, held, adjoint, tnew, snew, psel, qsel)

    def products(g, total):
        left, right = [], []
        for u in range(ROWS):
            i = g * ROWS + u
            left.append(jnp.concatenate([tcur[i], tnew[i]], axis=0))
            right.append(jnp.concatenate([sprev[i], scur[i]], axis=0).T)
        return total + nn(jnp.concatenate(left, axis=1), jnp.concatenate(right, axis=0))

    gram[...] = lax.fori_loop(0, steps, products, jnp.zeros(gram.shape, F32))


def local_products(sz, meta, col, tiles, turned, fields):
    gram = shape((2 * sz.chan, 2 * sz.chan), F32)
    return call(
        functools.partial(local_kernel, sz),
        [SMEM] * 2 + [VMEM] * 6,
        [VMEM] * 5,
        [sz.field, sz.field, sz.picked, sz.picked, gram],
        [pltpu.VMEM((sz.blocks, sz.chan, sz.blk), F32)] * 2,
        4 * sz.blocks * sz.nz * sz.chan * sz.blk * sz.blk,
        12 << 20,
        24,
    )(meta, col, tiles, turned, *fields)


def early_rows_kernel(sz, *refs):
    meta, col, tiles, turned, tcur, scur, tprev, _ = refs[:8]
    tnew, held, summed = refs[8:]
    clear_sums(sz, summed)
    cut = part_steps(meta[sz.live]) // 2
    arrays = (tiles, turned, tcur, scur, tprev)
    row_products(sz, col, 0, cut, ROWS_PART, arrays, tnew, held, summed)


def late_rows_kernel(sz, *refs):
    meta, col, tiles, turned, tcur, scur, tprev, sprev = refs[:8]
    tnew, held, summed, snew, psel, qsel = refs[12:]
    steps = part_steps(meta[sz.live])
    arrays = (tiles, turned, tcur, scur, tprev)
    row_products(sz, col, steps // 2, steps, ROWS_PART, arrays, tnew, held, summed)

    def adjoint(i):
        return 2.0 * summed[i] - sprev[i].astype(F32)

    finish_local(sz, meta, held, adjoint, tnew, snew, psel, qsel)


def part_products(sz, meta, col, tiles, turned, fields, before, token):
    sums = shape((sz.blocks, sz.chan, sz.blk), F32)
    args = [meta, col, tiles, turned, *fields]
    outs, aliases = [sz.field, sums, sums], {}
    if before is None:
        args[-1] = token
    else:
        aliases = {len(args) + k: k for k in range(3)}
        args += [*before, token]
        outs += [sz.field, sz.picked, sz.picked]
    return call(
        functools.partial(early_rows_kernel if before is None else late_rows_kernel, sz),
        [SMEM] * 2 + [VMEM] * (len(args) - 2),
        [VMEM] * len(outs),
        outs,
        [],
        2 * sz.blocks * sz.nz * sz.chan * sz.blk * sz.blk,
        6 << 20,
        8,
        aliases,
    )(*args)


def add_coupled(sz, scale, meta, got, across, psel, qsel, pacc, qacc, which):
    for j in range(sz.pairs):
        pacc[j] = psel[j]
        qacc[j] = qsel[j]
    some = [(r, h, j) for r, h, j in sz.couplings() if r in which]
    terms = {j: nn(got[r][sz.forward_part(h), :], across[j]) for r, h, j in some}
    for r, h, j in some:
        terms[j] = (scale * meta[sz.flags + r].astype(F32)) * terms[j]
        spot = meta[sz.first_row + j]
        pacc[spot] = pacc[spot] + terms[j]
        spot = meta[sz.first_send + j]
        qacc[spot] = qacc[spot] + scale * got[r][sz.adjoint_part(h), :].astype(F32)
    return terms


def correct_kernel(sz, axis, *refs):
    meta, across, psel, qsel, gram0, gram, sold = refs[:7]
    got, refs = refs[7 : 7 + sz.rounds], refs[7 + sz.rounds :]
    pacc, qacc, keep_half, give_half, whole = refs
    which = range(sz.rounds)
    terms = add_coupled(sz, 2.0, meta, got, across, psel, qsel, pacc, qacc, which)
    left = jnp.concatenate([terms[j].astype(BF16) for j in range(sz.pairs)], axis=1)
    right = [sold[meta[sz.rows + j]].T for j in range(sz.pairs)]
    extra = nn(left, jnp.concatenate(right, axis=0))
    one, two = pl.ds(0, sz.chan), pl.ds(sz.chan, sz.chan)
    whole[one, one] = gram0[...]
    whole[two, one] = gram[one, one]
    whole[two, two] = gram[one, two]
    whole[one, two] = gram[two, two] + extra
    odd = lax.rem(lax.axis_index(axis), 2)
    keep_half[...] = whole[pl.ds(pl.multiple_of(odd * sz.chan, sz.chan), sz.chan), :]
    give_half[...] = whole[pl.ds(pl.multiple_of((1 - odd) * sz.chan, sz.chan), sz.chan), :]


def correct(sz, axis, meta, across, picked, got, gram0, gram, sold):
    args = [meta, across, *picked, gram0, gram, sold, *got]
    half = shape((sz.chan, 2 * sz.chan), F32)
    return call(
        functools.partial(correct_kernel, sz, axis),
        [SMEM] + [VMEM] * (len(args) - 1),
        [VMEM] * 4,
        [sz.picked, sz.picked, half, half],
        [pltpu.VMEM((2 * sz.chan, 2 * sz.chan), F32)],
        4 * sz.pairs * sz.chan * sz.blk * sz.blk,
        3 << 20,
        8,
    )(*args)


def patch(sz, meta, cross, tnew, snew, pacc, qacc, pays):
    for j in range(sz.pairs):
        tnew[meta[sz.rows + j]] = pacc[meta[sz.first_row + j]].astype(BF16)
        snew[meta[sz.sends + j]] = qacc[meta[sz.first_send + j]].astype(BF16)
    fill_pays(sz, meta, tnew, snew, cross, pays)


def start_kernel(sz, *refs):
    meta, cross, _, _, across, psel, qsel = refs[:7]
    got, refs = refs[7 : 7 + sz.rounds], refs[7 + sz.rounds :]
    tnew, snew = refs[:2]
    pacc, qacc = refs[-2:]
    add_coupled(sz, 1.0, meta, got, across, psel, qsel, pacc, qacc, range(sz.rounds))
    patch(sz, meta, cross, tnew, snew, pacc, qacc, refs[2:-2])


def join_kernel(sz, *refs):
    meta, cross, _, _, pacc, qacc, tnew, snew = refs[:8]
    patch(sz, meta, cross, tnew, snew, pacc, qacc, refs[8:])


def join(sz, meta, cross, base, rest, first):
    args = [meta, cross, *base, *rest]
    outs = [sz.field, sz.field] + [sz.pay] * sz.rounds
    outs = call(
        functools.partial(start_kernel if first else join_kernel, sz),
        [SMEM] + [VMEM] * (len(args) - 1),
        [VMEM] * len(outs),
        outs,
        [pltpu.VMEM(sz.picked.shape, F32)] * 2 if first else [],
        2 * sz.pairs * sz.chan * sz.blk * sz.blk,
        5 << 20,
        8,
        {2: 0, 3: 1},
    )(*args)
    return outs[0], outs[1], outs[2:]


def output_weights(weight):
    wide = [weight[k].astype(F32) for k in range(weight.shape[0])]
    ahead = jnp.concatenate([w.T for w in wide], axis=1).astype(BF16)
    back = jnp.concatenate(wide, axis=1).astype(BF16)
    return ahead, back


def output_block(sz, left, fields, held, spot):
    value = nn(left[...], jnp.concatenate(fields, axis=0)).astype(BF16)
    for t in range(sz.chan // SUB):
        held[(t,) + spot if len(spot) == 1 else (spot[1], t)] = value[t * SUB : (t + 1) * SUB]


def output_kernel(sz, low, *refs):
    forward, adjoint = refs[:4], refs[4:8]
    if low == 0:
        weight, ahead, back, held_out, held_grad = refs[8], *refs[10:]
        wide_ahead, wide_back = output_weights(weight)
        ahead[...] = wide_ahead
        back[...] = wide_back
        copies = []
    else:
        ahead, back, before_out, before_grad = refs[8:12]
        held_out, held_grad, out4, grad4, sem = refs[13:]
        part = pl.ds(0, low)
        copies = [
            pltpu.make_async_copy(before_out, out4.at[:, part], sem.at[0]),
            pltpu.make_async_copy(before_grad, grad4.at[:, part], sem.at[1]),
        ]
    for copy in copies:
        copy.start()

    def step(g, carry):
        for u in range(ROWS_PART):
            n = g * ROWS_PART + u
            output_block(sz, ahead, [f[low + n] for f in forward], held_out, (n,))
            output_block(sz, back, [f[low + n] for f in adjoint], held_grad, (n,))
        return carry

    lax.fori_loop(0, held_out.shape[1] // ROWS_PART, step, 0)
    for copy in copies:
        copy.wait()


def base_outputs(sz, low, high, forward, adjoint, rest, token, orders):
    groups = sz.chan // SUB
    held = shape((groups, high - low, SUB, sz.blk), BF16)
    whole = shape((groups, sz.blocks, SUB, sz.blk), BF16)
    wide = shape((sz.chan, orders * sz.chan), BF16)
    args = [*forward, *adjoint, *rest, token]
    outs = [wide, wide, held, held] if low == 0 else [held, held, whole, whole]
    return call(
        functools.partial(output_kernel, sz, low),
        [VMEM] * len(args),
        [VMEM] * 4 if low == 0 else [VMEM] * 2 + [HBM] * 2,
        outs,
        [pltpu.SemaphoreType.DMA((2,))] if low else [],
        16 * (high - low) * sz.chan * sz.chan * sz.blk,
        6 << 20,
        8,
    )(*args)


def fixed_blocks(sz, meta, which, weights, fields, last, held):
    for r, h, j in sz.couplings():
        if r in which:
            for side, spot, first in ((0, sz.rows, sz.first_row), (1, sz.sends, sz.first_send)):
                i = meta[spot + j]
                stack = [f[i] for f in fields[3 * side : 3 * side + 3]]
                stack.append(last[side][meta[first + j]].astype(BF16))
                output_block(sz, weights[side], stack, held[side], (None, j))


def fixed_copies(sz, meta, which, over, held, outs, sem):
    copies = []
    for side, spot in ((0, sz.rows), (1, sz.sends)):
        seen = [meta[spot + j] for r, h, j in sz.couplings() if r in over]
        for r, h, j in sz.couplings():
            if r in which:
                i = meta[spot + j]
                fresh = jnp.bool_(True)
                for other in seen:
                    fresh = jnp.logical_and(fresh, other != i)
                seen.append(i)
                copy = pltpu.make_async_copy(
                    held[side].at[j], outs[side].at[:, i], sem.at[side, j]
                )
                copies.append((fresh, copy))
    return copies


def early_kernel(sz, which, low, *refs):
    meta, across, psel, qsel = refs[:4]
    got, refs = dict(zip(which, refs[4 : 4 + len(which)])), refs[4 + len(which) :]
    weights, fields, high = refs[:2], refs[2:8], refs[8:10]
    pacc, qacc, held_out, held_grad, out4, grad4, sem_base = refs[13:]
    part = pl.ds(low, high[0].shape[1])
    base = [
        pltpu.make_async_copy(high[0], out4.at[:, part], sem_base.at[0]),
        pltpu.make_async_copy(high[1], grad4.at[:, part], sem_base.at[1]),
    ]
    for copy in base:
        copy.start()
    add_coupled(sz, 2.0, meta, got, across, psel, qsel, pacc, qacc, which)
    fixed_blocks(sz, meta, which, weights, fields, (pacc, qacc), (held_out, held_grad))
    for copy in base:
        copy.wait()


def early_outputs(sz, low, meta, across, picked, got, which, weights, fields, high, token, outs):
    args = [meta, across, *picked, *(got[r] for r in which), *weights, *fields, *high, token]
    whole = [shape(out.shape, BF16) for out in outs]
    held = shape((sz.pairs, sz.chan // SUB, SUB, sz.blk), BF16)
    return call(
        functools.partial(early_kernel, sz, which, low),
        [SMEM] + [VMEM] * (len(args) - 1) + [HBM] * 2,
        [VMEM] * 4 + [HBM] * 2,
        [sz.picked, sz.picked, held, held] + whole,
        [pltpu.SemaphoreType.DMA((2,))],
        8 * sz.pairs * sz.chan * sz.blk * sz.blk,
        4 << 20,
        8,
        {len(args): 4, len(args) + 1: 5},
    )(*args, *outs)


def fix_kernel(sz, axis, early, late, *refs):
    meta, across, psel, qsel = refs[:4]
    got, refs = dict(zip(late, refs[4 : 4 + len(late)])), refs[4 + len(late) :]
    weights, fields, fixed = refs[:2], refs[2:8], refs[8:10]
    mine, theirs = refs[10:12]
    out4, grad4, grad_w, pacc, qacc, held_out, held_grad, total, sem_out, sem_w = refs[14:]
    held, outs = (held_out, held_grad), (out4, grad4)
    odd = lax.rem(lax.axis_index(axis), 2) == 1
    top = jnp.where(odd, theirs[...], mine[...])
    low = jnp.where(odd, mine[...], theirs[...])
    zeroth, first = top[:, : sz.chan], low[:, : sz.chan]
    total[0] = zeroth
    total[1] = first
    total[2] = 2.0 * low[:, sz.chan :] - zeroth
    total[3] = 2.0 * top[:, sz.chan :] - first
    weight_copy = pltpu.make_async_copy(total, grad_w, sem_w)
    weight_copy.start()
    add_coupled(sz, 2.0, meta, got, across, psel, qsel, pacc, qacc, late)
    copies = fixed_copies(sz, meta, early, late, fixed, outs, sem_out)
    for fresh, copy in copies:
        pl.when(fresh)(copy.start)
    fixed_blocks(sz, meta, late, weights, fields, (pacc, qacc), held)
    last = fixed_copies(sz, meta, late, [], held, outs, sem_out)
    for fresh, copy in last:
        pl.when(fresh)(copy.start)
    for fresh, copy in copies + last:
        pl.when(fresh)(copy.wait)
    weight_copy.wait()


def fix_outputs(
    sz, axis, meta, across, picked, got, early, late, weights, fields, fixed, mine, theirs, outs
):
    args = [meta, across, *picked, *(got[r] for r in late), *weights, *fields, *fixed]
    args += [mine, theirs]
    whole = [shape(out.shape, BF16) for out in outs]
    held = pltpu.VMEM((sz.pairs, sz.chan // SUB, SUB, sz.blk), BF16)
    total = (4, sz.chan, sz.chan)
    return call(
        functools.partial(fix_kernel, sz, axis, early, late),
        [SMEM] + [VMEM] * (len(args) - 1) + [HBM] * 2,
        [HBM] * 3,
        whole + [shape(total, F32)],
        [pltpu.VMEM(sz.picked.shape, F32)] * 2
        + [held, held, pltpu.VMEM(total, F32)]
        + [pltpu.SemaphoreType.DMA((2, sz.pairs)), pltpu.SemaphoreType.DMA],
        8 * len(late) * sz.hb * sz.chan * sz.blk * sz.blk,
        2 << 20,
        8,
        {len(args): 0, len(args) + 1: 1},
    )(*args, *outs)


def add_kernel(gated, inputs, *refs):
    mine, theirs = refs[:2]
    outs = refs[inputs:]
    if gated:
        outs[2][...] = refs[2][...]
    outs[0][...] = mine[...] + theirs[...]
    if len(outs) > 1:
        outs[1][...] = jnp.zeros(outs[1].shape, F32)


def add(mine, theirs, pay, after, last=False):
    outs = [shape(mine.shape, F32)] + ([] if last else [TOKEN])
    args = [mine, theirs]
    if pay is not None:
        outs.append(shape(pay.shape, BF16))
        args.append(pay)
    args += after
    return call(
        functools.partial(add_kernel, pay is not None, len(args)),
        [VMEM] * len(args),
        [VMEM] * len(outs),
        outs,
        [],
        mine.size,
        12 * mine.size,
        2,
    )(*args)


def from_partner(values, bit):
    count = lax.axis_size("dom")
    route = []
    for low in range(count):
        high = low | 1 << bit
        if high != low and high < count:
            route += [(low, high), (high, low)]
    return lax.ppermute(values, "dom", route)


def local(
    features,
    cheb_weight,
    lap_tiles,
    col_index,
    cross_tiles,
    send_index,
    row_index,
    pair_on,
    blk_live,
    cotangent,
):
    sz = Sizes(features, lap_tiles, cross_tiles)
    split = (sz.chan // SUB, SUB, sz.blocks, sz.blk)
    x4 = features.reshape(split).transpose(0, 2, 1, 3)
    u4 = cotangent.reshape(split).transpose(0, 2, 1, 3)
    coupling = cross_tiles.reshape(sz.pairs, sz.blk, sz.blk)
    send, row = send_index.transpose(0, 2, 1), row_index.transpose(0, 2, 1)

    packed = pack(sz, x4, u4, coupling, send, row, pair_on, blk_live, col_index.T)
    t0, s0, cross, across, meta, col = packed[:6]
    everyone = range(sz.rounds)
    got = [from_partner(pay, bit) for bit, pay in enumerate(packed[6:])]
    *base, psel, qsel, tiles, turned, gram0 = first_products(sz, meta, col, lap_tiles, t0, s0)
    t1, s1, pays = join(sz, meta, cross, base, [across, psel, qsel, *got], True)

    got = [from_partner(pay, bit) for bit, pay in enumerate(pays)]
    fields = (t1, s1, t0, s0)
    *base, psel, qsel, gram = local_products(sz, meta, col, tiles, turned, fields)
    *picked, mine, given = correct(
        sz, "dom", meta, across, (psel, qsel), got, gram0, gram, s1
    )
    theirs = from_partner(given, 0)
    t2, s2, pays = join(sz, meta, cross, base, picked, False)

    state = {}

    middle = sz.blocks // (2 * ROWS_PART) * ROWS_PART
    orders = cheb_weight.shape[0]

    def window_early_rows(token):
        fields = (t2, s2, t1, s1)
        state["part"] = part_products(sz, meta, col, tiles, turned, fields, None, token)
        return None

    def window_late_rows(token):
        fields = (t2, s2, t1, s1)
        t3, _, _, s3, *state["picked"] = part_products(
            sz, meta, col, tiles, turned, fields, state["part"], token
        )
        state["last"] = (t3, s3)
        return state["picked"][0]

    def window_low(token):
        t3, s3 = state["last"]
        *state["weights"], left, right = base_outputs(
            sz, 0, middle, (t0, t1, t2, t3), (s0, s1, s2, s3), [cheb_weight], token, orders
        )
        state["low"] = [left, right]
        return left

    def window_high(token):
        t3, s3 = state["last"]
        rest = state["weights"] + state["low"]
        left, right, out4, grad4 = base_outputs(
            sz, middle, sz.blocks, (t0, t1, t2, t3), (s0, s1, s2, s3), rest, token, orders
        )
        state["high"], state["outs"] = [left, right], [out4, grad4]
        return left

    windows = [window_early_rows, window_late_rows, window_low, window_high]
    bits = list(reversed(range(1, (lax.axis_size("dom") - 1).bit_length())))
    pays, got = list(pays), [None] * sz.rounds
    history = (t0, t1, t2, s0, s1, s2)
    got[0] = from_partner(pays[0], 0)
    early = [0] + [bit for bit in bits[:-1] if bit < sz.rounds]
    late = [bit for bit in everyone if bit not in early]
    far = pays[bits[0]] if bits[0] < sz.rounds else None
    mine, token, *rest = add(mine, theirs, far, [])
    held = [got[0]]
    for at, bit in enumerate(bits):
        if bit < sz.rounds:
            pays[bit] = rest[0]
        theirs = from_partner(mine, bit)
        if bit < sz.rounds:
            got[bit] = from_partner(pays[bit], bit)
        if at < len(windows):
            token = windows[at](token)
        last = at + 1 == len(bits)
        gated = not last and bits[at + 1] < sz.rounds
        after = ([] if token is None else [token]) + held
        held = [got[bit]] if bit < sz.rounds else []
        if last:
            (mine,) = add(mine, theirs, None, after, True)
        else:
            mine, token, *rest = add(mine, theirs, pays[bits[at + 1]] if gated else None, after)
    theirs = from_partner(mine, 0)
    *picked, left, right, out4, grad4 = early_outputs(
        sz,
        middle,
        meta,
        across,
        state["picked"],
        got,
        early,
        state["weights"],
        history,
        state["high"],
        mine,
        state["outs"],
    )
    out4, grad4, grad_w = fix_outputs(
        sz,
        "dom",
        meta,
        across,
        picked,
        got,
        early,
        late,
        state["weights"],
        history,
        [left, right],
        mine,
        theirs,
        [out4, grad4],
    )
    conv_out = out4.transpose(0, 2, 1, 3).reshape(features.shape)
    grad_x = grad4.transpose(0, 2, 1, 3).reshape(features.shape)
    return (conv_out, grad_x, grad_w)


def solution(mesh):
    in_specs = (
        P(None, "dom"),
        P(),
        P("dom", None, None, None),
        P("dom", None),
        P("dom", None, None, None, None),
        P("dom", None, None),
        P("dom", None, None),
        P("dom", None),
        P("dom"),
        P(None, "dom"),
    )
    out_specs = (P(None, "dom"), P(None, "dom"), P())
    return jax.shard_map(local, mesh=mesh, in_specs=in_specs, out_specs=out_specs, check_vma=False)
```

profile of v0, /device:TPU:0, one launch (start us, length us, event | category | flops | bytes accessed | tf_op | source)
XLA Modules:
  0.0 48.0 jit_solution(2526618172161678690)
XLA Ops:
  1.3 2.4 %shard_map.121 = (bf16[64,64,128]{2,1,0:T(8,128)(2,1)S(1)}, bf16[64,64,128]{2,1,0:T(8,128)(2,1)S(1)}, bf16[10,128,128]{2,1,0:T(8,128)(2,1)S(1)}, bf16[10,128,128...) custom-call(bf16[8,64,8,128]{3,2,1,0:T(8,128)(2,1)} %bitcast.18, ...), custom_call_target="tpu_custom_call" | custom-call | flops 1000 | bytes 4194304 | tf_op jit(solution)/shard_map/pallas_call | solution.py:144
  3.7 0.8 %collective-permute-start = (bf16[256,128]{1,0:T(8,128)(2,1)S(1)}, bf16[256,128]{1,0:T(8,128)(2,1)S(1)}, u32[]{:S(2)}, u32[]{:S(2)}) collective-permute-start(bf16[256,128]{1,0:T(8,128)(2,1)S(1)} %get-tuple-element.92), channel_id=1, source_target_pairs={{0,1},{1,0},{2,3},{3,2},{4,5},{5,4},{6,7},{7,6},{8,9},{9,8},{10,11... | collective-permute-start | bytes 196616 | tf_op jit(solution)/shard_map/ppermute | solution.py:682
  4.4 2.3 %collective-permute-start.1 = (bf16[256,128]{1,0:T(8,128)(2,1)S(1)}, bf16[256,128]{1,0:T(8,128)(2,1)S(1)}, u32[]{:S(2)}, u32[]{:S(2)}) collective-permute-start(bf16[256,128]{1,0:T(8,128)(2,1)S(1)} %get-tuple-element.93), channel_id=1, source_target_pairs={{0,2},{2,0},{1,3},{3,1},{4,6},{6,4},{5,7},{7,5},{8,10},{10,8},{9,1... | collective-permute-start | bytes 196616 | tf_op jit(solution)/shard_map/ppermute | solution.py:682
  6.8 1.7 %collective-permute-start.2 = (bf16[256,128]{1,0:T(8,128)(2,1)S(1)}, bf16[256,128]{1,0:T(8,128)(2,1)S(1)}, u32[]{:S(2)}, u32[]{:S(2)}) collective-permute-start(bf16[256,128]{1,0:T(8,128)(2,1)S(1)} %get-tuple-element.94), channel_id=1, source_target_pairs={{0,4},{4,0},{1,5},{5,1},{2,6},{6,2},{3,7},{7,3},{8,12},{12,8},{9,1... | collective-permute-start | bytes 196616 | tf_op jit(solution)/shard_map/ppermute | solution.py:682
  8.5 1.3 %collective-permute-start.3 = (bf16[256,128]{1,0:T(8,128)(2,1)S(1)}, bf16[256,128]{1,0:T(8,128)(2,1)S(1)}, u32[]{:S(2)}, u32[]{:S(2)}) collective-permute-start(bf16[256,128]{1,0:T(8,128)(2,1)S(1)} %get-tuple-element.95), channel_id=1, source_target_pairs={{0,8},{8,0},{1,9},{9,1},{2,10},{10,2},{3,11},{11,3},{4,12},{12,4},... | collective-permute-start | bytes 196616 | tf_op jit(solution)/shard_map/ppermute | solution.py:682
  9.7 2.6 %collective-permute-start.4 = (bf16[256,128]{1,0:T(8,128)(2,1)S(1)}, bf16[256,128]{1,0:T(8,128)(2,1)S(1)}, u32[]{:S(2)}, u32[]{:S(2)}) collective-permute-start(bf16[256,128]{1,0:T(8,128)(2,1)S(1)} %get-tuple-element.96), channel_id=1, source_target_pairs={{0,16},{16,0},{1,17},{17,1},{2,18},{18,2},{3,19},{19,3},{4,20},{20... | collective-permute-start | bytes 196616 | tf_op jit(solution)/shard_map/ppermute | solution.py:682
  12.3 4.6 %shard_map.122 = (bf16[64,64,128]{2,1,0:T(8,128)(2,1)S(1)}, bf16[64,64,128]{2,1,0:T(8,128)(2,1)S(1)}, f32[10,64,128]{2,1,0:T(8,128)S(1)}, f32[10,64,128]{2,1,0:T...) custom-call(s32[46]{0:T(128)S(4)} %get-tuple-element.80.refs_0_, ...), custom_call_target="tpu_custom_call" | custom-call | flops 805306368 | bytes 12582912 | tf_op jit(solution)/shard_map/pallas_call | solution.py:263
  16.9 0.0 collective-permute-done.refs_7_
  16.9 0.0 collective-permute-done.1.refs_8_
  16.9 0.0 collective-permute-done.3.refs_10_
  16.9 0.0 collective-permute-done.4.refs_11_
  16.9 0.3 shard_map.123
  17.3 0.1 collective-permute-start.5
  17.4 0.7 %collective-permute-start.6 = (bf16[256,128]{1,0:T(8,128)(2,1)S(1)}, bf16[256,128]{1,0:T(8,128)(2,1)S(1)}, u32[]{:S(2)}, u32[]{:S(2)}) collective-permute-start(bf16[256,128]{1,0:T(8,128)(2,1)S(1)} %get-tuple-element.106), channel_id=1, source_target_pairs={{0,2},{2,0},{1,3},{3,1},{4,6},{6,4},{5,7},{7,5},{8,10},{10,8},{9,1... | collective-permute-start | bytes 196616 | tf_op jit(solution)/shard_map/ppermute | solution.py:682
  18.1 0.3 collective-permute-start.7
  18.3 0.4 collective-permute-start.8
  18.8 1.2 %collective-permute-start.9 = (bf16[256,128]{1,0:T(8,128)(2,1)S(1)}, bf16[256,128]{1,0:T(8,128)(2,1)S(1)}, u32[]{:S(2)}, u32[]{:S(2)}) collective-permute-start(bf16[256,128]{1,0:T(8,128)(2,1)S(1)} %get-tuple-element.109), channel_id=1, source_target_pairs={{0,16},{16,0},{1,17},{17,1},{2,18},{18,2},{3,19},{19,3},{4,20},{20... | collective-permute-start | bytes 196616 | tf_op jit(solution)/shard_map/ppermute | solution.py:682
  19.9 4.5 %shard_map.124 = (bf16[64,64,128]{2,1,0:T(8,128)(2,1)S(1)}, bf16[64,64,128]{2,1,0:T(8,128)(2,1)S(1)}, f32[10,64,128]{2,1,0:T(8,128)S(1)}, f32[10,64,128]{2,1,0:T(8,128)S(1)}, f32[128,128]{1,0:T(8,128)S(1)}) custom-call(s32[46]{0:T(128)S(4)} %get-tuple-element.80.refs_0_, s32[3,64]{1,0:T(4,128)S(4)} %get-tuple-element.82.refs_1_, ...), custom_call_target="tpu_custom_call" | custom-call | flops 805306368 | bytes 12582912 | tf_op jit(solution)/shard_map/pallas_call | solution.py:323
  24.4 0.0 collective-permute-done.5.refs_7_
  24.5 0.0 collective-permute-done.7.refs_9_
  24.5 0.0 collective-permute-done.8.refs_10_
  24.5 0.7 %collective-permute-done.9.refs_11_ = bf16[256,128]{1,0:T(8,128)(2,1)S(1)} collective-permute-done((bf16[256,128]{1,0:T(8,128)(2,1)S(1)}, bf16[256,128]{1,0:T(8,128)(2,1)S(1)}, u32[]{:S(2)}, u32[]{:S(2)}) %collective-permute-start.9) | collective-permute-done | bytes 65568 | tf_op jit(solution)/shard_map/ppermute | solution.py:682
  25.2 0.5 shard_map.125
  25.7 0.1 collective-permute-start.10
  25.7 0.3 shard_map.126
  26.0 0.6 %collective-permute-start.12 = (bf16[256,128]{1,0:T(8,128)(2,1)S(1)}, bf16[256,128]{1,0:T(8,128)(2,1)S(1)}, u32[]{:S(2)}, u32[]{:S(2)}) collective-permute-start(bf16[256,128]{1,0:T(8,128)(2,1)S(1)} %get-tuple-element.123), channel_id=1, source_target_pairs={{0,1},{1,0},{2,3},{3,2},{4,5},{5,4},{6,7},{7,6},{8,9},{9,8},{10,11... | collective-permute-start | bytes 196616 | tf_op jit(solution)/shard_map/ppermute | solution.py:682
  26.6 0.4 collective-permute-done.10.refs_1_
  26.9 1.0 %collective-permute-start.11 = (f32[64,128]{1,0:T(8,128)S(1)}, f32[64,128]{1,0:T(8,128)S(1)}, u32[]{:S(2)}, u32[]{:S(2)}) collective-permute-start(f32[64,128]{1,0:T(8,128)S(1)} %get-tuple-element.121.refs_0_), channel_id=1, source_target_pairs={{0,16},{16,0},{1,17},{17,1},{2,18},{18,2},{3,19},{19,3},{4,20},{20... | collective-permute-start | bytes 98312 | tf_op jit(solution)/shard_map/ppermute | solution.py:682
  27.9 2.0 %collective-permute-start.13 = (bf16[256,128]{1,0:T(8,128)(2,1)S(1)}, bf16[256,128]{1,0:T(8,128)(2,1)S(1)}, u32[]{:S(2)}, u32[]{:S(2)}) collective-permute-start(bf16[256,128]{1,0:T(8,128)(2,1)S(1)} %get-tuple-element.127), channel_id=1, source_target_pairs={{0,16},{16,0},{1,17},{17,1},{2,18},{18,2},{3,19},{19,3},{4,20},{20... | collective-permute-start | bytes 196616 | tf_op jit(solution)/shard_map/ppermute | solution.py:682
  29.9 0.9 %shard_map.128 = (bf16[64,64,128]{2,1,0:T(8,128)(2,1)S(1)}, f32[64,64,128]{2,1,0:T(8,128)S(1)}, f32[64,64,128]{2,1,0:T(8,128)S(1)}) custom-call(s32[46]{0:T(128)S(4)} %get-tuple-element.80.refs_0_, s32[3,64]{1,0:T(4,128)S(4)} %get-tuple-element.82.refs_1_, bf16[64,3,128,128]{3,2,1,0:T(8,128)(2,1)S(1)} %get-tuple-element.85.refs_2_, ...), custom_call_target="tpu_custom_call" | custom-call | flops 402653184 | bytes 6291456 | tf_op jit(solution)/shard_map/pallas_call | solution.py:367
  30.9 0.0 collective-permute-done.12.refs_3_.refs_4_
  30.9 1.5 %collective-permute-done.11.refs_1_ = f32[64,128]{1,0:T(8,128)S(1)} collective-permute-done((f32[64,128]{1,0:T(8,128)S(1)}, f32[64,128]{1,0:T(8,128)S(1)}, u32[]{:S(2)}, u32[]{:S(2)}) %collective-permute-start.11) | collective-permute-done | bytes 32800 | tf_op jit(solution)/shard_map/ppermute | solution.py:682
  32.4 0.1 collective-permute-start.15
  32.5 2.0 %collective-permute-start.14 = (bf16[256,128]{1,0:T(8,128)(2,1)S(1)}, bf16[256,128]{1,0:T(8,128)(2,1)S(1)}, u32[]{:S(2)}, u32[]{:S(2)}) collective-permute-start(bf16[256,128]{1,0:T(8,128)(2,1)S(1)} %get-tuple-element.128), channel_id=1, source_target_pairs={{0,8},{8,0},{1,9},{9,1},{2,10},{10,2},{3,11},{11,3},{4,12},{12,4},... | collective-permute-start | bytes 196616 | tf_op jit(solution)/shard_map/ppermute | solution.py:682
  34.5 2.0 %shard_map.130 = (bf16[64,64,128]{2,1,0:T(8,128)(2,1)S(1)}, f32[64,64,128]{2,1,0:T(8,128)S(1)}, f32[64,64,128]{2,1,0:T(8,128)S(1)}, bf16[64,64,128]{2,1,0:T(8,12...) custom-call(s32[46]{0:T(128)S(4)} %get-tuple-element.80.refs_0_, ...), custom_call_target="tpu_custom_call", output_to_operand_aliasing={{0}: (8, {}), {1}: (9, {}), {2}: (10, {})} | custom-call | flops 402653184 | bytes 6291456 | tf_op jit(solution)/shard_map/pallas_call | solution.py:367
  36.5 0.0 collective-permute-done.13.refs_4_.refs_5_
  36.6 0.6 %collective-permute-start.17 = (f32[64,128]{1,0:T(8,128)S(1)}, f32[64,128]{1,0:T(8,128)S(1)}, u32[]{:S(2)}, u32[]{:S(2)}) collective-permute-start(f32[64,128]{1,0:T(8,128)S(1)} %get-tuple-element.139.refs_0_), channel_id=1, source_target_pairs={{0,4},{4,0},{1,5},{5,1},{2,6},{6,2},{3,7},{7,3},{8,12},{12,8},{9,1... | collective-permute-start | bytes 98312 | tf_op jit(solution)/shard_map/ppermute | solution.py:682
  37.2 1.5 %collective-permute-start.16 = (bf16[256,128]{1,0:T(8,128)(2,1)S(1)}, bf16[256,128]{1,0:T(8,128)(2,1)S(1)}, u32[]{:S(2)}, u32[]{:S(2)}) collective-permute-start(bf16[256,128]{1,0:T(8,128)(2,1)S(1)} %get-tuple-element.131), channel_id=1, source_target_pairs={{0,4},{4,0},{1,5},{5,1},{2,6},{6,2},{3,7},{7,3},{8,12},{12,8},{9,1... | collective-permute-start | bytes 196616 | tf_op jit(solution)/shard_map/ppermute | solution.py:682
  38.7 1.1 %shard_map.132 = (bf16[64,256]{1,0:T(8,128)(2,1)S(1)}, bf16[64,256]{1,0:T(8,128)(2,1)S(1)}, bf16[8,32,8,128]{3,2,1,0:T(8,128)(2,1)S(1)}, bf16[8,32,8,128]{3,2,1,0:T(8,128)(2,1)S(1)}) custom-call(bf16[64,64,128]{2,1,0:T(8,128)(2,1)S(1)} %get-tuple-element.83.refs_3_.refs_6_.refs_0_.refs_10_.refs_7_, ...), custom_call_target="tpu_custom_call" | custom-call | flops 268435456 | bytes 6291456 | tf_op jit(solution)/shard_map/pallas_call | solution.py:518
  39.7 0.8 %collective-permute-done.17.refs_1_ = f32[64,128]{1,0:T(8,128)S(1)} collective-permute-done((f32[64,128]{1,0:T(8,128)S(1)}, f32[64,128]{1,0:T(8,128)S(1)}, u32[]{:S(2)}, u32[]{:S(2)}) %collective-permute-start.17) | collective-permute-done | bytes 32800 | tf_op jit(solution)/shard_map/ppermute | solution.py:682
  40.6 2.0 %collective-permute-start.18 = (f32[64,128]{1,0:T(8,128)S(1)}, f32[64,128]{1,0:T(8,128)S(1)}, u32[]{:S(2)}, u32[]{:S(2)}) collective-permute-start(f32[64,128]{1,0:T(8,128)S(1)} %get-tuple-element.144.refs_0_), channel_id=1, source_target_pairs={{0,2},{2,0},{1,3},{3,1},{4,6},{6,4},{5,7},{7,5},{8,10},{10,8},{9,1... | collective-permute-start | bytes 98312 | tf_op jit(solution)/shard_map/ppermute | solution.py:682
  42.6 0.1 collective-permute-start.19
  42.7 1.0 %shard_map.134 = (bf16[8,32,8,128]{3,2,1,0:T(8,128)(2,1)S(1)}, bf16[8,32,8,128]{3,2,1,0:T(8,128)(2,1)S(1)}, bf16[8,64,8,128]{3,2,1,0:T(8,128)(2,1)}, bf16[8,64,8,128]{3,2,1,0:T(8,128)(2,1)}) custom-call(bf16[64,64,128]{2,1,0:T(8,128)(2,1)S(1)} %get-tuple-element.83.refs_3_.refs_6_.refs_0_.refs_10_.refs_7_, ...), custom_call_target="tpu_custom_call" | custom-call | flops 268435456 | bytes 6291456 | tf_op jit(solution)/shard_map/pallas_call | solution.py:518
  43.6 0.9 %collective-permute-done.18.refs_1_ = f32[64,128]{1,0:T(8,128)S(1)} collective-permute-done((f32[64,128]{1,0:T(8,128)S(1)}, f32[64,128]{1,0:T(8,128)S(1)}, u32[]{:S(2)}, u32[]{:S(2)}) %collective-permute-start.18) | collective-permute-done | bytes 32800 | tf_op jit(solution)/shard_map/ppermute | solution.py:682
  44.6 0.1 collective-permute-start.20
  44.6 1.3 %shard_map.136 = (f32[10,64,128]{2,1,0:T(8,128)S(1)}, f32[10,64,128]{2,1,0:T(8,128)S(1)}, bf16[10,8,8,128]{3,2,1,0:T(8,128)(2,1)S(1)}, bf16[10,8,8,128]{3,2,1,0:...) custom-call(s32[46]{0:T(128)S(4)} %get-tuple-element.80.refs_0_, ...), custom_call_target="tpu_custom_call", output_to_operand_aliasing={{4}: (19, {}), {5}: (20, {})} | custom-call | flops 83886080 | bytes 4194304 | tf_op jit(solution)/shard_map/pallas_call | solution.py:580
  46.0 0.9 %collective-permute-done.19.refs_4_ = bf16[256,128]{1,0:T(8,128)(2,1)S(1)} collective-permute-done((bf16[256,128]{1,0:T(8,128)(2,1)S(1)}, bf16[256,128]{1,0:T(8,128)(2,1)S(1)}, u32[]{:S(2)}, u32[]{:S(2)}) %collective-permute-start.19) | collective-permute-done | bytes 65568 | tf_op jit(solution)/shard_map/ppermute | solution.py:682
  46.8 1.1 %shard_map.137 = (bf16[8,64,8,128]{3,2,1,0:T(8,128)(2,1)}, bf16[8,64,8,128]{3,2,1,0:T(8,128)(2,1)}, f32[4,64,64]{2,1,0:T(8,128)}) custom-call(s32[46]{0:T(128)S(4)} %get-tuple-element.80.refs_0_, bf16[10,128,128]{2,1,0:T(8,128)(2,1)S(1)} %get-tuple-element.81.refs_4_.refs_1_, ...), custom_call_target="tpu_custom_call", output_to_operand_aliasing={{0}: (17, {}), {1}: (18, {})} | custom-call | flops 16777216 | bytes 2097152 | tf_op jit(solution)/shard_map/pallas_call | solution.py:631
  (13 shorter events, 0.1 us)
Async XLA Ops:
  3.7 13.2 %collective-permute-start = (bf16[256,128]{1,0:T(8,128)(2,1)S(1)}, bf16[256,128]{1,0:T(8,128)(2,1)S(1)}, u32[]{:S(2)}, u32[]{:S(2)}) collective-permute-start(bf16[256,128]{1,0:T(8,128)(2,1)S(1)} %get-tuple-element.92), channel_id=1, source_target_pairs={{0,1},{1,0},{2,3},{3,2},{4,5},{5,4},{6,7},{7,6},{8,9},{9,8},{10,11... | collective-permute-start | bytes 196616 | tf_op jit(solution)/shard_map/ppermute | solution.py:682
  4.4 12.5 %collective-permute-start.1 = (bf16[256,128]{1,0:T(8,128)(2,1)S(1)}, bf16[256,128]{1,0:T(8,128)(2,1)S(1)}, u32[]{:S(2)}, u32[]{:S(2)}) collective-permute-start(bf16[256,128]{1,0:T(8,128)(2,1)S(1)} %get-tuple-element.93), channel_id=1, source_target_pairs={{0,2},{2,0},{1,3},{3,1},{4,6},{6,4},{5,7},{7,5},{8,10},{10,8},{9,1... | collective-permute-start | bytes 196616 | tf_op jit(solution)/shard_map/ppermute | solution.py:682
  6.8 10.1 %collective-permute-start.2 = (bf16[256,128]{1,0:T(8,128)(2,1)S(1)}, bf16[256,128]{1,0:T(8,128)(2,1)S(1)}, u32[]{:S(2)}, u32[]{:S(2)}) collective-permute-start(bf16[256,128]{1,0:T(8,128)(2,1)S(1)} %get-tuple-element.94), channel_id=1, source_target_pairs={{0,4},{4,0},{1,5},{5,1},{2,6},{6,2},{3,7},{7,3},{8,12},{12,8},{9,1... | collective-permute-start | bytes 196616 | tf_op jit(solution)/shard_map/ppermute | solution.py:682
  8.5 8.5 %collective-permute-start.3 = (bf16[256,128]{1,0:T(8,128)(2,1)S(1)}, bf16[256,128]{1,0:T(8,128)(2,1)S(1)}, u32[]{:S(2)}, u32[]{:S(2)}) collective-permute-start(bf16[256,128]{1,0:T(8,128)(2,1)S(1)} %get-tuple-element.95), channel_id=1, source_target_pairs={{0,8},{8,0},{1,9},{9,1},{2,10},{10,2},{3,11},{11,3},{4,12},{12,4},... | collective-permute-start | bytes 196616 | tf_op jit(solution)/shard_map/ppermute | solution.py:682
  9.7 7.2 %collective-permute-start.4 = (bf16[256,128]{1,0:T(8,128)(2,1)S(1)}, bf16[256,128]{1,0:T(8,128)(2,1)S(1)}, u32[]{:S(2)}, u32[]{:S(2)}) collective-permute-start(bf16[256,128]{1,0:T(8,128)(2,1)S(1)} %get-tuple-element.96), channel_id=1, source_target_pairs={{0,16},{16,0},{1,17},{17,1},{2,18},{18,2},{3,19},{19,3},{4,20},{20... | collective-permute-start | bytes 196616 | tf_op jit(solution)/shard_map/ppermute | solution.py:682
  17.3 7.1 %collective-permute-start.5 = (bf16[256,128]{1,0:T(8,128)(2,1)S(1)}, bf16[256,128]{1,0:T(8,128)(2,1)S(1)}, u32[]{:S(2)}, u32[]{:S(2)}) collective-permute-start(bf16[256,128]{1,0:T(8,128)(2,1)S(1)} %get-tuple-element.105), channel_id=1, source_target_pairs={{0,1},{1,0},{2,3},{3,2},{4,5},{5,4},{6,7},{7,6},{8,9},{9,8},{10,11... | collective-permute-start | bytes 196616 | tf_op jit(solution)/shard_map/ppermute | solution.py:682
  17.4 7.1 %collective-permute-start.6 = (bf16[256,128]{1,0:T(8,128)(2,1)S(1)}, bf16[256,128]{1,0:T(8,128)(2,1)S(1)}, u32[]{:S(2)}, u32[]{:S(2)}) collective-permute-start(bf16[256,128]{1,0:T(8,128)(2,1)S(1)} %get-tuple-element.106), channel_id=1, source_target_pairs={{0,2},{2,0},{1,3},{3,1},{4,6},{6,4},{5,7},{7,5},{8,10},{10,8},{9,1... | collective-permute-start | bytes 196616 | tf_op jit(solution)/shard_map/ppermute | solution.py:682
  18.1 6.4 %collective-permute-start.7 = (bf16[256,128]{1,0:T(8,128)(2,1)S(1)}, bf16[256,128]{1,0:T(8,128)(2,1)S(1)}, u32[]{:S(2)}, u32[]{:S(2)}) collective-permute-start(bf16[256,128]{1,0:T(8,128)(2,1)S(1)} %get-tuple-element.107), channel_id=1, source_target_pairs={{0,4},{4,0},{1,5},{5,1},{2,6},{6,2},{3,7},{7,3},{8,12},{12,8},{9,1... | collective-permute-start | bytes 196616 | tf_op jit(solution)/shard_map/ppermute | solution.py:682
  18.3 6.1 %collective-permute-start.8 = (bf16[256,128]{1,0:T(8,128)(2,1)S(1)}, bf16[256,128]{1,0:T(8,128)(2,1)S(1)}, u32[]{:S(2)}, u32[]{:S(2)}) collective-permute-start(bf16[256,128]{1,0:T(8,128)(2,1)S(1)} %get-tuple-element.108), channel_id=1, source_target_pairs={{0,8},{8,0},{1,9},{9,1},{2,10},{10,2},{3,11},{11,3},{4,12},{12,4},... | collective-permute-start | bytes 196616 | tf_op jit(solution)/shard_map/ppermute | solution.py:682
  18.8 6.4 %collective-permute-start.9 = (bf16[256,128]{1,0:T(8,128)(2,1)S(1)}, bf16[256,128]{1,0:T(8,128)(2,1)S(1)}, u32[]{:S(2)}, u32[]{:S(2)}) collective-permute-start(bf16[256,128]{1,0:T(8,128)(2,1)S(1)} %get-tuple-element.109), channel_id=1, source_target_pairs={{0,16},{16,0},{1,17},{17,1},{2,18},{18,2},{3,19},{19,3},{4,20},{20... | collective-permute-start | bytes 196616 | tf_op jit(solution)/shard_map/ppermute | solution.py:682
  25.7 1.3 %collective-permute-start.10 = (f32[64,128]{1,0:T(8,128)S(1)}, f32[64,128]{1,0:T(8,128)S(1)}, u32[]{:S(2)}, u32[]{:S(2)}) collective-permute-start(f32[64,128]{1,0:T(8,128)S(1)} %get-tuple-element.115), channel_id=1, source_target_pairs={{0,1},{1,0},{2,3},{3,2},{4,5},{5,4},{6,7},{7,6},{8,9},{9,8},{10,11... | collective-permute-start | bytes 98312 | tf_op jit(solution)/shard_map/ppermute | solution.py:682
  26.0 4.9 %collective-permute-start.12 = (bf16[256,128]{1,0:T(8,128)(2,1)S(1)}, bf16[256,128]{1,0:T(8,128)(2,1)S(1)}, u32[]{:S(2)}, u32[]{:S(2)}) collective-permute-start(bf16[256,128]{1,0:T(8,128)(2,1)S(1)} %get-tuple-element.123), channel_id=1, source_target_pairs={{0,1},{1,0},{2,3},{3,2},{4,5},{5,4},{6,7},{7,6},{8,9},{9,8},{10,11... | collective-permute-start | bytes 196616 | tf_op jit(solution)/shard_map/ppermute | solution.py:682
  26.9 5.4 %collective-permute-start.11 = (f32[64,128]{1,0:T(8,128)S(1)}, f32[64,128]{1,0:T(8,128)S(1)}, u32[]{:S(2)}, u32[]{:S(2)}) collective-permute-start(f32[64,128]{1,0:T(8,128)S(1)} %get-tuple-element.121.refs_0_), channel_id=1, source_target_pairs={{0,16},{16,0},{1,17},{17,1},{2,18},{18,2},{3,19},{19,3},{4,20},{20... | collective-permute-start | bytes 98312 | tf_op jit(solution)/shard_map/ppermute | solution.py:682
  27.9 8.6 %collective-permute-start.13 = (bf16[256,128]{1,0:T(8,128)(2,1)S(1)}, bf16[256,128]{1,0:T(8,128)(2,1)S(1)}, u32[]{:S(2)}, u32[]{:S(2)}) collective-permute-start(bf16[256,128]{1,0:T(8,128)(2,1)S(1)} %get-tuple-element.127), channel_id=1, source_target_pairs={{0,16},{16,0},{1,17},{17,1},{2,18},{18,2},{3,19},{19,3},{4,20},{20... | collective-permute-start | bytes 196616 | tf_op jit(solution)/shard_map/ppermute | solution.py:682
  32.4 4.1 %collective-permute-start.15 = (f32[64,128]{1,0:T(8,128)S(1)}, f32[64,128]{1,0:T(8,128)S(1)}, u32[]{:S(2)}, u32[]{:S(2)}) collective-permute-start(f32[64,128]{1,0:T(8,128)S(1)} %get-tuple-element.129.refs_0_), channel_id=1, source_target_pairs={{0,8},{8,0},{1,9},{9,1},{2,10},{10,2},{3,11},{11,3},{4,12},{12,4},... | collective-permute-start | bytes 98312 | tf_op jit(solution)/shard_map/ppermute | solution.py:682
  32.5 8.1 %collective-permute-start.14 = (bf16[256,128]{1,0:T(8,128)(2,1)S(1)}, bf16[256,128]{1,0:T(8,128)(2,1)S(1)}, u32[]{:S(2)}, u32[]{:S(2)}) collective-permute-start(bf16[256,128]{1,0:T(8,128)(2,1)S(1)} %get-tuple-element.128), channel_id=1, source_target_pairs={{0,8},{8,0},{1,9},{9,1},{2,10},{10,2},{3,11},{11,3},{4,12},{12,4},... | collective-permute-start | bytes 196616 | tf_op jit(solution)/shard_map/ppermute | solution.py:682
  34.5 4.2 %copy-start = (bf16[4,64,64]{2,1,0:T(8,128)(2,1)S(1)}, bf16[4,64,64]{2,1,0:T(8,128)(2,1)}, u32[]{:S(2)}) copy-start(bf16[4,64,64]{2,1,0:T(8,128)(2,1)} %refs_8_.1) | copy-start | bytes 98308
  36.6 4.0 %collective-permute-start.17 = (f32[64,128]{1,0:T(8,128)S(1)}, f32[64,128]{1,0:T(8,128)S(1)}, u32[]{:S(2)}, u32[]{:S(2)}) collective-permute-start(f32[64,128]{1,0:T(8,128)S(1)} %get-tuple-element.139.refs_0_), channel_id=1, source_target_pairs={{0,4},{4,0},{1,5},{5,1},{2,6},{6,2},{3,7},{7,3},{8,12},{12,8},{9,1... | collective-permute-start | bytes 98312 | tf_op jit(solution)/shard_map/ppermute | solution.py:682
  37.2 7.4 %collective-permute-start.16 = (bf16[256,128]{1,0:T(8,128)(2,1)S(1)}, bf16[256,128]{1,0:T(8,128)(2,1)S(1)}, u32[]{:S(2)}, u32[]{:S(2)}) collective-permute-start(bf16[256,128]{1,0:T(8,128)(2,1)S(1)} %get-tuple-element.131), channel_id=1, source_target_pairs={{0,4},{4,0},{1,5},{5,1},{2,6},{6,2},{3,7},{7,3},{8,12},{12,8},{9,1... | collective-permute-start | bytes 196616 | tf_op jit(solution)/shard_map/ppermute | solution.py:682
  40.6 4.0 %collective-permute-start.18 = (f32[64,128]{1,0:T(8,128)S(1)}, f32[64,128]{1,0:T(8,128)S(1)}, u32[]{:S(2)}, u32[]{:S(2)}) collective-permute-start(f32[64,128]{1,0:T(8,128)S(1)} %get-tuple-element.144.refs_0_), channel_id=1, source_target_pairs={{0,2},{2,0},{1,3},{3,1},{4,6},{6,4},{5,7},{7,5},{8,10},{10,8},{9,1... | collective-permute-start | bytes 98312 | tf_op jit(solution)/shard_map/ppermute | solution.py:682
  42.6 4.3 %collective-permute-start.19 = (bf16[256,128]{1,0:T(8,128)(2,1)S(1)}, bf16[256,128]{1,0:T(8,128)(2,1)S(1)}, u32[]{:S(2)}, u32[]{:S(2)}) collective-permute-start(bf16[256,128]{1,0:T(8,128)(2,1)S(1)} %get-tuple-element.149), channel_id=1, source_target_pairs={{0,2},{2,0},{1,3},{3,1},{4,6},{6,4},{5,7},{7,5},{8,10},{10,8},{9,1... | collective-permute-start | bytes 196616 | tf_op jit(solution)/shard_map/ppermute | solution.py:682
  44.6 1.4 %collective-permute-start.20 = (f32[64,128]{1,0:T(8,128)S(1)}, f32[64,128]{1,0:T(8,128)S(1)}, u32[]{:S(2)}, u32[]{:S(2)}) collective-permute-start(f32[64,128]{1,0:T(8,128)S(1)} %shard_map.135.refs_18_.refs_15_), channel_id=1, source_target_pairs={{0,1},{1,0},{2,3},{3,2},{4,5},{5,4},{6,7},{7,6},{8,9},{9,8},{10,11... | collective-permute-start | bytes 98312 | tf_op jit(solution)/shard_map/ppermute | solution.py:682
where the time goes:
time: 48.1 us; the launch traced here: 48 us
  starting transfers between devices  21.2 us (44%)
  Pallas kernels  20 us (42%)
  waiting for transfers between devices  5.2 us (11%)
  between operations  1.51 us (3%)
    ppermute x21, starting transfers between devices, from_partner(): return lax.ppermute(values, 'dom', route)  21.2 us
    ppermute x21, waiting for transfers between devices, from_partner(): return lax.ppermute(values, 'dom', route)  5.2 us
    pallas_call x1, Pallas kernels, first_products(): call(functools.partial(first_kernel, sz), [SMEM, SMEM, HBM, VMEM, VMEM],...  4.57 us
    pallas_call x1, Pallas kernels, local_products(): call(functools.partial(local_kernel, sz), [SMEM] * 2 + [VMEM] * 6, [VMEM]...  4.48 us
    pallas_call x2, Pallas kernels, part_products(): call(functools.partial(early_rows_kernel if before is None else late_rows...  2.98 us
    pallas_call x1, Pallas kernels, pack(): call(functools.partial(pack_kernel, sz), [HBM] * 6 + [SMEM, HBM], [VMEM]...  2.37 us
    pallas_call x2, Pallas kernels, base_outputs(): call(functools.partial(output_kernel, sz, low), [VMEM] * len(args), [VMEM...  2.04 us
    pallas_call x1, Pallas kernels, early_outputs(): call(functools.partial(early_kernel, sz, which, low), [SMEM] + [VMEM] * (...  1.31 us
  transfers between devices with their start and end apart: 21, of which 6 were waited for; matrix products, arithmetic and copies ran while one was open for 0% of the time, Pallas kernels for 33%

commit v1 on v0

--- a/solution.py
+++ b/solution.py
@@ -704,7 +704,9 @@
     packed = pack(sz, x4, u4, coupling, send, row, pair_on, blk_live, col_index.T)
     t0, s0, cross, across, meta, col = packed[:6]
     everyone = range(sz.rounds)
-    got = [from_partner(pay, bit) for bit, pay in enumerate(packed[6:])]
+    got = []
+    for bit, pay in enumerate(packed[6:]):
+        got.append(from_partner(pay, bit))
     *base, psel, qsel, tiles, turned, gram0 = first_products(sz, meta, col, lap_tiles, t0, s0)
     t1, s1, pays = join(sz, meta, cross, base, [across, psel, qsel, *got], True)
 
@@ -759,8 +761,7 @@
     got[0] = from_partner(pays[0], 0)
     early = [0] + [bit for bit in bits[:-1] if bit < sz.rounds]
     late = [bit for bit in everyone if bit not in early]
-    far = pays[bits[0]] if bits[0] < sz.rounds else None
-    mine, token, *rest = add(mine, theirs, far, [])
+    mine, token, *rest = add(mine, theirs, pays[bits[0]] if bits[0] < sz.rounds else None, [])
     held = [got[0]]
     for at, bit in enumerate(bits):
         if bit < sz.rounds:

time: 48.1 us -> 48.1 us (level)
  no operation moved by 1% of the time
where the time goes in v1:
time: 48.1 us; the launch traced here: 48 us
  starting transfers between devices  21.2 us (44%)
  Pallas kernels  20 us (42%)
  waiting for transfers between devices  5.2 us (11%)
  between operations  1.51 us (3%)
    ppermute x21, starting transfers between devices, from_partner(): return lax.ppermute(values, 'dom', route)  21.2 us
    ppermute x21, waiting for transfers between devices, from_partner(): return lax.ppermute(values, 'dom', route)  5.2 us
    pallas_call x1, Pallas kernels, first_products(): call(functools.partial(first_kernel, sz), [SMEM, SMEM, HBM, VMEM, VMEM],...  4.57 us
    pallas_call x1, Pallas kernels, local_products(): call(functools.partial(local_kernel, sz), [SMEM] * 2 + [VMEM] * 6, [VMEM]...  4.48 us
    pallas_call x2, Pallas kernels, part_products(): call(functools.partial(early_rows_kernel if before is None else late_rows...  2.98 us
    pallas_call x1, Pallas kernels, pack(): call(functools.partial(pack_kernel, sz), [HBM] * 6 + [SMEM, HBM], [VMEM]...  2.37 us
    pallas_call x2, Pallas kernels, base_outputs(): call(functools.partial(output_kernel, sz, low), [VMEM] * len(args), [VMEM...  2.04 us
    pallas_call x1, Pallas kernels, early_outputs(): call(functools.partial(early_kernel, sz, which, low), [SMEM] + [VMEM] * (...  1.31 us
  transfers between devices with their start and end apart: 21, of which 6 were waited for; matrix products, arithmetic and copies ran while one was open for 0% of the time, Pallas kernels for 33%

profile of v1, /device:TPU:0, one launch (start us, length us, event | category | flops | bytes accessed | tf_op | source)
XLA Modules:
  0.0 48.0 jit_solution(2526618172161678690)
XLA Ops:
  1.3 2.4 %shard_map.121 = (bf16[64,64,128]{2,1,0:T(8,128)(2,1)S(1)}, bf16[64,64,128]{2,1,0:T(8,128)(2,1)S(1)}, bf16[10,128,128]{2,1,0:T(8,128)(2,1)S(1)}, bf16[10,128,128...) custom-call(bf16[8,64,8,128]{3,2,1,0:T(8,128)(2,1)} %bitcast.18, ...), custom_call_target="tpu_custom_call" | custom-call | flops 1000 | bytes 4194304 | tf_op jit(solution)/shard_map/pallas_call | solution.py:144
  3.7 0.8 %collective-permute-start = (bf16[256,128]{1,0:T(8,128)(2,1)S(1)}, bf16[256,128]{1,0:T(8,128)(2,1)S(1)}, u32[]{:S(2)}, u32[]{:S(2)}) collective-permute-start(bf16[256,128]{1,0:T(8,128)(2,1)S(1)} %get-tuple-element.92), channel_id=1, source_target_pairs={{0,1},{1,0},{2,3},{3,2},{4,5},{5,4},{6,7},{7,6},{8,9},{9,8},{10,11... | collective-permute-start | bytes 196616 | tf_op jit(solution)/shard_map/ppermute | solution.py:682
  4.4 2.3 %collective-permute-start.1 = (bf16[256,128]{1,0:T(8,128)(2,1)S(1)}, bf16[256,128]{1,0:T(8,128)(2,1)S(1)}, u32[]{:S(2)}, u32[]{:S(2)}) collective-permute-start(bf16[256,128]{1,0:T(8,128)(2,1)S(1)} %get-tuple-element.93), channel_id=1, source_target_pairs={{0,2},{2,0},{1,3},{3,1},{4,6},{6,4},{5,7},{7,5},{8,10},{10,8},{9,1... | collective-permute-start | bytes 196616 | tf_op jit(solution)/shard_map/ppermute | solution.py:682
  6.8 1.7 %collective-permute-start.2 = (bf16[256,128]{1,0:T(8,128)(2,1)S(1)}, bf16[256,128]{1,0:T(8,128)(2,1)S(1)}, u32[]{:S(2)}, u32[]{:S(2)}) collective-permute-start(bf16[256,128]{1,0:T(8,128)(2,1)S(1)} %get-tuple-element.94), channel_id=1, source_target_pairs={{0,4},{4,0},{1,5},{5,1},{2,6},{6,2},{3,7},{7,3},{8,12},{12,8},{9,1... | collective-permute-start | bytes 196616 | tf_op jit(solution)/shard_map/ppermute | solution.py:682
  8.5 1.3 %collective-permute-start.3 = (bf16[256,128]{1,0:T(8,128)(2,1)S(1)}, bf16[256,128]{1,0:T(8,128)(2,1)S(1)}, u32[]{:S(2)}, u32[]{:S(2)}) collective-permute-start(bf16[256,128]{1,0:T(8,128)(2,1)S(1)} %get-tuple-element.95), channel_id=1, source_target_pairs={{0,8},{8,0},{1,9},{9,1},{2,10},{10,2},{3,11},{11,3},{4,12},{12,4},... | collective-permute-start | bytes 196616 | tf_op jit(solution)/shard_map/ppermute | solution.py:682
  9.7 2.6 %collective-permute-start.4 = (bf16[256,128]{1,0:T(8,128)(2,1)S(1)}, bf16[256,128]{1,0:T(8,128)(2,1)S(1)}, u32[]{:S(2)}, u32[]{:S(2)}) collective-permute-start(bf16[256,128]{1,0:T(8,128)(2,1)S(1)} %get-tuple-element.96), channel_id=1, source_target_pairs={{0,16},{16,0},{1,17},{17,1},{2,18},{18,2},{3,19},{19,3},{4,20},{20... | collective-permute-start | bytes 196616 | tf_op jit(solution)/shard_map/ppermute | solution.py:682
  12.3 4.6 %shard_map.122 = (bf16[64,64,128]{2,1,0:T(8,128)(2,1)S(1)}, bf16[64,64,128]{2,1,0:T(8,128)(2,1)S(1)}, f32[10,64,128]{2,1,0:T(8,128)S(1)}, f32[10,64,128]{2,1,0:T...) custom-call(s32[46]{0:T(128)S(4)} %get-tuple-element.80.refs_0_, ...), custom_call_target="tpu_custom_call" | custom-call | flops 805306368 | bytes 12582912 | tf_op jit(solution)/shard_map/pallas_call | solution.py:263
  16.9 0.0 collective-permute-done.refs_7_
  16.9 0.0 collective-permute-done.1.refs_8_
  16.9 0.0 collective-permute-done.3.refs_10_
  16.9 0.0 collective-permute-done.4.refs_11_
  16.9 0.3 shard_map.123
  17.3 0.1 collective-permute-start.5
  17.4 0.7 %collective-permute-start.6 = (bf16[256,128]{1,0:T(8,128)(2,1)S(1)}, bf16[256,128]{1,0:T(8,128)(2,1)S(1)}, u32[]{:S(2)}, u32[]{:S(2)}) collective-permute-start(bf16[256,128]{1,0:T(8,128)(2,1)S(1)} %get-tuple-element.106), channel_id=1, source_target_pairs={{0,2},{2,0},{1,3},{3,1},{4,6},{6,4},{5,7},{7,5},{8,10},{10,8},{9,1... | collective-permute-start | bytes 196616 | tf_op jit(solution)/shard_map/ppermute | solution.py:682
  18.1 0.3 collective-permute-start.7
  18.3 0.4 collective-permute-start.8
  18.8 1.2 %collective-permute-start.9 = (bf16[256,128]{1,0:T(8,128)(2,1)S(1)}, bf16[256,128]{1,0:T(8,128)(2,1)S(1)}, u32[]{:S(2)}, u32[]{:S(2)}) collective-permute-start(bf16[256,128]{1,0:T(8,128)(2,1)S(1)} %get-tuple-element.109), channel_id=1, source_target_pairs={{0,16},{16,0},{1,17},{17,1},{2,18},{18,2},{3,19},{19,3},{4,20},{20... | collective-permute-start | bytes 196616 | tf_op jit(solution)/shard_map/ppermute | solution.py:682
  19.9 4.5 %shard_map.124 = (bf16[64,64,128]{2,1,0:T(8,128)(2,1)S(1)}, bf16[64,64,128]{2,1,0:T(8,128)(2,1)S(1)}, f32[10,64,128]{2,1,0:T(8,128)S(1)}, f32[10,64,128]{2,1,0:T(8,128)S(1)}, f32[128,128]{1,0:T(8,128)S(1)}) custom-call(s32[46]{0:T(128)S(4)} %get-tuple-element.80.refs_0_, s32[3,64]{1,0:T(4,128)S(4)} %get-tuple-element.82.refs_1_, ...), custom_call_target="tpu_custom_call" | custom-call | flops 805306368 | bytes 12582912 | tf_op jit(solution)/shard_map/pallas_call | solution.py:323
  24.4 0.0 collective-permute-done.5.refs_7_
  24.5 0.0 collective-permute-done.7.refs_9_
  24.5 0.0 collective-permute-done.8.refs_10_
  24.5 0.7 %collective-permute-done.9.refs_11_ = bf16[256,128]{1,0:T(8,128)(2,1)S(1)} collective-permute-done((bf16[256,128]{1,0:T(8,128)(2,1)S(1)}, bf16[256,128]{1,0:T(8,128)(2,1)S(1)}, u32[]{:S(2)}, u32[]{:S(2)}) %collective-permute-start.9) | collective-permute-done | bytes 65568 | tf_op jit(solution)/shard_map/ppermute | solution.py:682
  25.2 0.5 shard_map.125
  25.7 0.1 collective-permute-start.10
  25.7 0.3 shard_map.126
  26.0 0.6 %collective-permute-start.12 = (bf16[256,128]{1,0:T(8,128)(2,1)S(1)}, bf16[256,128]{1,0:T(8,128)(2,1)S(1)}, u32[]{:S(2)}, u32[]{:S(2)}) collective-permute-start(bf16[256,128]{1,0:T(8,128)(2,1)S(1)} %get-tuple-element.123), channel_id=1, source_target_pairs={{0,1},{1,0},{2,3},{3,2},{4,5},{5,4},{6,7},{7,6},{8,9},{9,8},{10,11... | collective-permute-start | bytes 196616 | tf_op jit(solution)/shard_map/ppermute | solution.py:682
  26.6 0.4 collective-permute-done.10.refs_1_
  26.9 1.0 %collective-permute-start.11 = (f32[64,128]{1,0:T(8,128)S(1)}, f32[64,128]{1,0:T(8,128)S(1)}, u32[]{:S(2)}, u32[]{:S(2)}) collective-permute-start(f32[64,128]{1,0:T(8,128)S(1)} %get-tuple-element.121.refs_0_), channel_id=1, source_target_pairs={{0,16},{16,0},{1,17},{17,1},{2,18},{18,2},{3,19},{19,3},{4,20},{20... | collective-permute-start | bytes 98312 | tf_op jit(solution)/shard_map/ppermute | solution.py:682
  27.9 2.0 %collective-permute-start.13 = (bf16[256,128]{1,0:T(8,128)(2,1)S(1)}, bf16[256,128]{1,0:T(8,128)(2,1)S(1)}, u32[]{:S(2)}, u32[]{:S(2)}) collective-permute-start(bf16[256,128]{1,0:T(8,128)(2,1)S(1)} %get-tuple-element.127), channel_id=1, source_target_pairs={{0,16},{16,0},{1,17},{17,1},{2,18},{18,2},{3,19},{19,3},{4,20},{20... | collective-permute-start | bytes 196616 | tf_op jit(solution)/shard_map/ppermute | solution.py:682
  29.9 0.9 %shard_map.128 = (bf16[64,64,128]{2,1,0:T(8,128)(2,1)S(1)}, f32[64,64,128]{2,1,0:T(8,128)S(1)}, f32[64,64,128]{2,1,0:T(8,128)S(1)}) custom-call(s32[46]{0:T(128)S(4)} %get-tuple-element.80.refs_0_, s32[3,64]{1,0:T(4,128)S(4)} %get-tuple-element.82.refs_1_, bf16[64,3,128,128]{3,2,1,0:T(8,128)(2,1)S(1)} %get-tuple-element.85.refs_2_, ...), custom_call_target="tpu_custom_call" | custom-call | flops 402653184 | bytes 6291456 | tf_op jit(solution)/shard_map/pallas_call | solution.py:367
  30.9 0.0 collective-permute-done.12.refs_3_.refs_4_
  30.9 1.5 %collective-permute-done.11.refs_1_ = f32[64,128]{1,0:T(8,128)S(1)} collective-permute-done((f32[64,128]{1,0:T(8,128)S(1)}, f32[64,128]{1,0:T(8,128)S(1)}, u32[]{:S(2)}, u32[]{:S(2)}) %collective-permute-start.11) | collective-permute-done | bytes 32800 | tf_op jit(solution)/shard_map/ppermute | solution.py:682
  32.4 0.1 collective-permute-start.15
  32.5 2.0 %collective-permute-start.14 = (bf16[256,128]{1,0:T(8,128)(2,1)S(1)}, bf16[256,128]{1,0:T(8,128)(2,1)S(1)}, u32[]{:S(2)}, u32[]{:S(2)}) collective-permute-start(bf16[256,128]{1,0:T(8,128)(2,1)S(1)} %get-tuple-element.128), channel_id=1, source_target_pairs={{0,8},{8,0},{1,9},{9,1},{2,10},{10,2},{3,11},{11,3},{4,12},{12,4},... | collective-permute-start | bytes 196616 | tf_op jit(solution)/shard_map/ppermute | solution.py:682
  34.5 2.0 %shard_map.130 = (bf16[64,64,128]{2,1,0:T(8,128)(2,1)S(1)}, f32[64,64,128]{2,1,0:T(8,128)S(1)}, f32[64,64,128]{2,1,0:T(8,128)S(1)}, bf16[64,64,128]{2,1,0:T(8,12...) custom-call(s32[46]{0:T(128)S(4)} %get-tuple-element.80.refs_0_, ...), custom_call_target="tpu_custom_call", output_to_operand_aliasing={{0}: (8, {}), {1}: (9, {}), {2}: (10, {})} | custom-call | flops 402653184 | bytes 6291456 | tf_op jit(solution)/shard_map/pallas_call | solution.py:367
  36.5 0.0 collective-permute-done.13.refs_4_.refs_5_
  36.6 0.6 %collective-permute-start.17 = (f32[64,128]{1,0:T(8,128)S(1)}, f32[64,128]{1,0:T(8,128)S(1)}, u32[]{:S(2)}, u32[]{:S(2)}) collective-permute-start(f32[64,128]{1,0:T(8,128)S(1)} %get-tuple-element.139.refs_0_), channel_id=1, source_target_pairs={{0,4},{4,0},{1,5},{5,1},{2,6},{6,2},{3,7},{7,3},{8,12},{12,8},{9,1... | collective-permute-start | bytes 98312 | tf_op jit(solution)/shard_map/ppermute | solution.py:682
  37.2 1.5 %collective-permute-start.16 = (bf16[256,128]{1,0:T(8,128)(2,1)S(1)}, bf16[256,128]{1,0:T(8,128)(2,1)S(1)}, u32[]{:S(2)}, u32[]{:S(2)}) collective-permute-start(bf16[256,128]{1,0:T(8,128)(2,1)S(1)} %get-tuple-element.131), channel_id=1, source_target_pairs={{0,4},{4,0},{1,5},{5,1},{2,6},{6,2},{3,7},{7,3},{8,12},{12,8},{9,1... | collective-permute-start | bytes 196616 | tf_op jit(solution)/shard_map/ppermute | solution.py:682
  38.7 1.1 %shard_map.132 = (bf16[64,256]{1,0:T(8,128)(2,1)S(1)}, bf16[64,256]{1,0:T(8,128)(2,1)S(1)}, bf16[8,32,8,128]{3,2,1,0:T(8,128)(2,1)S(1)}, bf16[8,32,8,128]{3,2,1,0:T(8,128)(2,1)S(1)}) custom-call(bf16[64,64,128]{2,1,0:T(8,128)(2,1)S(1)} %get-tuple-element.83.refs_3_.refs_6_.refs_0_.refs_10_.refs_7_, ...), custom_call_target="tpu_custom_call" | custom-call | flops 268435456 | bytes 6291456 | tf_op jit(solution)/shard_map/pallas_call | solution.py:518
  39.7 0.8 %collective-permute-done.17.refs_1_ = f32[64,128]{1,0:T(8,128)S(1)} collective-permute-done((f32[64,128]{1,0:T(8,128)S(1)}, f32[64,128]{1,0:T(8,128)S(1)}, u32[]{:S(2)}, u32[]{:S(2)}) %collective-permute-start.17) | collective-permute-done | bytes 32800 | tf_op jit(solution)/shard_map/ppermute | solution.py:682
  40.6 2.0 %collective-permute-start.18 = (f32[64,128]{1,0:T(8,128)S(1)}, f32[64,128]{1,0:T(8,128)S(1)}, u32[]{:S(2)}, u32[]{:S(2)}) collective-permute-start(f32[64,128]{1,0:T(8,128)S(1)} %get-tuple-element.144.refs_0_), channel_id=1, source_target_pairs={{0,2},{2,0},{1,3},{3,1},{4,6},{6,4},{5,7},{7,5},{8,10},{10,8},{9,1... | collective-permute-start | bytes 98312 | tf_op jit(solution)/shard_map/ppermute | solution.py:682
  42.6 0.1 collective-permute-start.19
  42.7 1.0 %shard_map.134 = (bf16[8,32,8,128]{3,2,1,0:T(8,128)(2,1)S(1)}, bf16[8,32,8,128]{3,2,1,0:T(8,128)(2,1)S(1)}, bf16[8,64,8,128]{3,2,1,0:T(8,128)(2,1)}, bf16[8,64,8,128]{3,2,1,0:T(8,128)(2,1)}) custom-call(bf16[64,64,128]{2,1,0:T(8,128)(2,1)S(1)} %get-tuple-element.83.refs_3_.refs_6_.refs_0_.refs_10_.refs_7_, ...), custom_call_target="tpu_custom_call" | custom-call | flops 268435456 | bytes 6291456 | tf_op jit(solution)/shard_map/pallas_call | solution.py:518
  43.6 0.9 %collective-permute-done.18.refs_1_ = f32[64,128]{1,0:T(8,128)S(1)} collective-permute-done((f32[64,128]{1,0:T(8,128)S(1)}, f32[64,128]{1,0:T(8,128)S(1)}, u32[]{:S(2)}, u32[]{:S(2)}) %collective-permute-start.18) | collective-permute-done | bytes 32800 | tf_op jit(solution)/shard_map/ppermute | solution.py:682
  44.6 0.1 collective-permute-start.20
  44.6 1.3 %shard_map.136 = (f32[10,64,128]{2,1,0:T(8,128)S(1)}, f32[10,64,128]{2,1,0:T(8,128)S(1)}, bf16[10,8,8,128]{3,2,1,0:T(8,128)(2,1)S(1)}, bf16[10,8,8,128]{3,2,1,0:...) custom-call(s32[46]{0:T(128)S(4)} %get-tuple-element.80.refs_0_, ...), custom_call_target="tpu_custom_call", output_to_operand_aliasing={{4}: (19, {}), {5}: (20, {})} | custom-call | flops 83886080 | bytes 4194304 | tf_op jit(solution)/shard_map/pallas_call | solution.py:580
  46.0 0.9 %collective-permute-done.19.refs_4_ = bf16[256,128]{1,0:T(8,128)(2,1)S(1)} collective-permute-done((bf16[256,128]{1,0:T(8,128)(2,1)S(1)}, bf16[256,128]{1,0:T(8,128)(2,1)S(1)}, u32[]{:S(2)}, u32[]{:S(2)}) %collective-permute-start.19) | collective-permute-done | bytes 65568 | tf_op jit(solution)/shard_map/ppermute | solution.py:682
  46.8 1.1 %shard_map.137 = (bf16[8,64,8,128]{3,2,1,0:T(8,128)(2,1)}, bf16[8,64,8,128]{3,2,1,0:T(8,128)(2,1)}, f32[4,64,64]{2,1,0:T(8,128)}) custom-call(s32[46]{0:T(128)S(4)} %get-tuple-element.80.refs_0_, bf16[10,128,128]{2,1,0:T(8,128)(2,1)S(1)} %get-tuple-element.81.refs_4_.refs_1_, ...), custom_call_target="tpu_custom_call", output_to_operand_aliasing={{0}: (17, {}), {1}: (18, {})} | custom-call | flops 16777216 | bytes 2097152 | tf_op jit(solution)/shard_map/pallas_call | solution.py:631
  (13 shorter events, 0.1 us)
Async XLA Ops:
  3.7 13.2 %collective-permute-start = (bf16[256,128]{1,0:T(8,128)(2,1)S(1)}, bf16[256,128]{1,0:T(8,128)(2,1)S(1)}, u32[]{:S(2)}, u32[]{:S(2)}) collective-permute-start(bf16[256,128]{1,0:T(8,128)(2,1)S(1)} %get-tuple-element.92), channel_id=1, source_target_pairs={{0,1},{1,0},{2,3},{3,2},{4,5},{5,4},{6,7},{7,6},{8,9},{9,8},{10,11... | collective-permute-start | bytes 196616 | tf_op jit(solution)/shard_map/ppermute | solution.py:682
  4.4 12.5 %collective-permute-start.1 = (bf16[256,128]{1,0:T(8,128)(2,1)S(1)}, bf16[256,128]{1,0:T(8,128)(2,1)S(1)}, u32[]{:S(2)}, u32[]{:S(2)}) collective-permute-start(bf16[256,128]{1,0:T(8,128)(2,1)S(1)} %get-tuple-element.93), channel_id=1, source_target_pairs={{0,2},{2,0},{1,3},{3,1},{4,6},{6,4},{5,7},{7,5},{8,10},{10,8},{9,1... | collective-permute-start | bytes 196616 | tf_op jit(solution)/shard_map/ppermute | solution.py:682
  6.8 10.1 %collective-permute-start.2 = (bf16[256,128]{1,0:T(8,128)(2,1)S(1)}, bf16[256,128]{1,0:T(8,128)(2,1)S(1)}, u32[]{:S(2)}, u32[]{:S(2)}) collective-permute-start(bf16[256,128]{1,0:T(8,128)(2,1)S(1)} %get-tuple-element.94), channel_id=1, source_target_pairs={{0,4},{4,0},{1,5},{5,1},{2,6},{6,2},{3,7},{7,3},{8,12},{12,8},{9,1... | collective-permute-start | bytes 196616 | tf_op jit(solution)/shard_map/ppermute | solution.py:682
  8.5 8.5 %collective-permute-start.3 = (bf16[256,128]{1,0:T(8,128)(2,1)S(1)}, bf16[256,128]{1,0:T(8,128)(2,1)S(1)}, u32[]{:S(2)}, u32[]{:S(2)}) collective-permute-start(bf16[256,128]{1,0:T(8,128)(2,1)S(1)} %get-tuple-element.95), channel_id=1, source_target_pairs={{0,8},{8,0},{1,9},{9,1},{2,10},{10,2},{3,11},{11,3},{4,12},{12,4},... | collective-permute-start | bytes 196616 | tf_op jit(solution)/shard_map/ppermute | solution.py:682
  9.7 7.2 %collective-permute-start.4 = (bf16[256,128]{1,0:T(8,128)(2,1)S(1)}, bf16[256,128]{1,0:T(8,128)(2,1)S(1)}, u32[]{:S(2)}, u32[]{:S(2)}) collective-permute-start(bf16[256,128]{1,0:T(8,128)(2,1)S(1)} %get-tuple-element.96), channel_id=1, source_target_pairs={{0,16},{16,0},{1,17},{17,1},{2,18},{18,2},{3,19},{19,3},{4,20},{20... | collective-permute-start | bytes 196616 | tf_op jit(solution)/shard_map/ppermute | solution.py:682
  17.3 7.1 %collective-permute-start.5 = (bf16[256,128]{1,0:T(8,128)(2,1)S(1)}, bf16[256,128]{1,0:T(8,128)(2,1)S(1)}, u32[]{:S(2)}, u32[]{:S(2)}) collective-permute-start(bf16[256,128]{1,0:T(8,128)(2,1)S(1)} %get-tuple-element.105), channel_id=1, source_target_pairs={{0,1},{1,0},{2,3},{3,2},{4,5},{5,4},{6,7},{7,6},{8,9},{9,8},{10,11... | collective-permute-start | bytes 196616 | tf_op jit(solution)/shard_map/ppermute | solution.py:682
  17.4 7.1 %collective-permute-start.6 = (bf16[256,128]{1,0:T(8,128)(2,1)S(1)}, bf16[256,128]{1,0:T(8,128)(2,1)S(1)}, u32[]{:S(2)}, u32[]{:S(2)}) collective-permute-start(bf16[256,128]{1,0:T(8,128)(2,1)S(1)} %get-tuple-element.106), channel_id=1, source_target_pairs={{0,2},{2,0},{1,3},{3,1},{4,6},{6,4},{5,7},{7,5},{8,10},{10,8},{9,1... | collective-permute-start | bytes 196616 | tf_op jit(solution)/shard_map/ppermute | solution.py:682
  18.1 6.4 %collective-permute-start.7 = (bf16[256,128]{1,0:T(8,128)(2,1)S(1)}, bf16[256,128]{1,0:T(8,128)(2,1)S(1)}, u32[]{:S(2)}, u32[]{:S(2)}) collective-permute-start(bf16[256,128]{1,0:T(8,128)(2,1)S(1)} %get-tuple-element.107), channel_id=1, source_target_pairs={{0,4},{4,0},{1,5},{5,1},{2,6},{6,2},{3,7},{7,3},{8,12},{12,8},{9,1... | collective-permute-start | bytes 196616 | tf_op jit(solution)/shard_map/ppermute | solution.py:682
  18.3 6.1 %collective-permute-start.8 = (bf16[256,128]{1,0:T(8,128)(2,1)S(1)}, bf16[256,128]{1,0:T(8,128)(2,1)S(1)}, u32[]{:S(2)}, u32[]{:S(2)}) collective-permute-start(bf16[256,128]{1,0:T(8,128)(2,1)S(1)} %get-tuple-element.108), channel_id=1, source_target_pairs={{0,8},{8,0},{1,9},{9,1},{2,10},{10,2},{3,11},{11,3},{4,12},{12,4},... | collective-permute-start | bytes 196616 | tf_op jit(solution)/shard_map/ppermute | solution.py:682
  18.8 6.4 %collective-permute-start.9 = (bf16[256,128]{1,0:T(8,128)(2,1)S(1)}, bf16[256,128]{1,0:T(8,128)(2,1)S(1)}, u32[]{:S(2)}, u32[]{:S(2)}) collective-permute-start(bf16[256,128]{1,0:T(8,128)(2,1)S(1)} %get-tuple-element.109), channel_id=1, source_target_pairs={{0,16},{16,0},{1,17},{17,1},{2,18},{18,2},{3,19},{19,3},{4,20},{20... | collective-permute-start | bytes 196616 | tf_op jit(solution)/shard_map/ppermute | solution.py:682
  25.7 1.3 %collective-permute-start.10 = (f32[64,128]{1,0:T(8,128)S(1)}, f32[64,128]{1,0:T(8,128)S(1)}, u32[]{:S(2)}, u32[]{:S(2)}) collective-permute-start(f32[64,128]{1,0:T(8,128)S(1)} %get-tuple-element.115), channel_id=1, source_target_pairs={{0,1},{1,0},{2,3},{3,2},{4,5},{5,4},{6,7},{7,6},{8,9},{9,8},{10,11... | collective-permute-start | bytes 98312 | tf_op jit(solution)/shard_map/ppermute | solution.py:682
  26.0 4.9 %collective-permute-start.12 = (bf16[256,128]{1,0:T(8,128)(2,1)S(1)}, bf16[256,128]{1,0:T(8,128)(2,1)S(1)}, u32[]{:S(2)}, u32[]{:S(2)}) collective-permute-start(bf16[256,128]{1,0:T(8,128)(2,1)S(1)} %get-tuple-element.123), channel_id=1, source_target_pairs={{0,1},{1,0},{2,3},{3,2},{4,5},{5,4},{6,7},{7,6},{8,9},{9,8},{10,11... | collective-permute-start | bytes 196616 | tf_op jit(solution)/shard_map/ppermute | solution.py:682
  26.9 5.4 %collective-permute-start.11 = (f32[64,128]{1,0:T(8,128)S(1)}, f32[64,128]{1,0:T(8,128)S(1)}, u32[]{:S(2)}, u32[]{:S(2)}) collective-permute-start(f32[64,128]{1,0:T(8,128)S(1)} %get-tuple-element.121.refs_0_), channel_id=1, source_target_pairs={{0,16},{16,0},{1,17},{17,1},{2,18},{18,2},{3,19},{19,3},{4,20},{20... | collective-permute-start | bytes 98312 | tf_op jit(solution)/shard_map/ppermute | solution.py:682
  27.9 8.6 %collective-permute-start.13 = (bf16[256,128]{1,0:T(8,128)(2,1)S(1)}, bf16[256,128]{1,0:T(8,128)(2,1)S(1)}, u32[]{:S(2)}, u32[]{:S(2)}) collective-permute-start(bf16[256,128]{1,0:T(8,128)(2,1)S(1)} %get-tuple-element.127), channel_id=1, source_target_pairs={{0,16},{16,0},{1,17},{17,1},{2,18},{18,2},{3,19},{19,3},{4,20},{20... | collective-permute-start | bytes 196616 | tf_op jit(solution)/shard_map/ppermute | solution.py:682
  32.4 4.1 %collective-permute-start.15 = (f32[64,128]{1,0:T(8,128)S(1)}, f32[64,128]{1,0:T(8,128)S(1)}, u32[]{:S(2)}, u32[]{:S(2)}) collective-permute-start(f32[64,128]{1,0:T(8,128)S(1)} %get-tuple-element.129.refs_0_), channel_id=1, source_target_pairs={{0,8},{8,0},{1,9},{9,1},{2,10},{10,2},{3,11},{11,3},{4,12},{12,4},... | collective-permute-start | bytes 98312 | tf_op jit(solution)/shard_map/ppermute | solution.py:682
  32.5 8.1 %collective-permute-start.14 = (bf16[256,128]{1,0:T(8,128)(2,1)S(1)}, bf16[256,128]{1,0:T(8,128)(2,1)S(1)}, u32[]{:S(2)}, u32[]{:S(2)}) collective-permute-start(bf16[256,128]{1,0:T(8,128)(2,1)S(1)} %get-tuple-element.128), channel_id=1, source_target_pairs={{0,8},{8,0},{1,9},{9,1},{2,10},{10,2},{3,11},{11,3},{4,12},{12,4},... | collective-permute-start | bytes 196616 | tf_op jit(solution)/shard_map/ppermute | solution.py:682
  34.5 4.2 %copy-start = (bf16[4,64,64]{2,1,0:T(8,128)(2,1)S(1)}, bf16[4,64,64]{2,1,0:T(8,128)(2,1)}, u32[]{:S(2)}) copy-start(bf16[4,64,64]{2,1,0:T(8,128)(2,1)} %refs_8_.1) | copy-start | bytes 98308
  36.6 4.0 %collective-permute-start.17 = (f32[64,128]{1,0:T(8,128)S(1)}, f32[64,128]{1,0:T(8,128)S(1)}, u32[]{:S(2)}, u32[]{:S(2)}) collective-permute-start(f32[64,128]{1,0:T(8,128)S(1)} %get-tuple-element.139.refs_0_), channel_id=1, source_target_pairs={{0,4},{4,0},{1,5},{5,1},{2,6},{6,2},{3,7},{7,3},{8,12},{12,8},{9,1... | collective-permute-start | bytes 98312 | tf_op jit(solution)/shard_map/ppermute | solution.py:682
  37.2 7.4 %collective-permute-start.16 = (bf16[256,128]{1,0:T(8,128)(2,1)S(1)}, bf16[256,128]{1,0:T(8,128)(2,1)S(1)}, u32[]{:S(2)}, u32[]{:S(2)}) collective-permute-start(bf16[256,128]{1,0:T(8,128)(2,1)S(1)} %get-tuple-element.131), channel_id=1, source_target_pairs={{0,4},{4,0},{1,5},{5,1},{2,6},{6,2},{3,7},{7,3},{8,12},{12,8},{9,1... | collective-permute-start | bytes 196616 | tf_op jit(solution)/shard_map/ppermute | solution.py:682
  40.6 4.0 %collective-permute-start.18 = (f32[64,128]{1,0:T(8,128)S(1)}, f32[64,128]{1,0:T(8,128)S(1)}, u32[]{:S(2)}, u32[]{:S(2)}) collective-permute-start(f32[64,128]{1,0:T(8,128)S(1)} %get-tuple-element.144.refs_0_), channel_id=1, source_target_pairs={{0,2},{2,0},{1,3},{3,1},{4,6},{6,4},{5,7},{7,5},{8,10},{10,8},{9,1... | collective-permute-start | bytes 98312 | tf_op jit(solution)/shard_map/ppermute | solution.py:682
  42.6 4.3 %collective-permute-start.19 = (bf16[256,128]{1,0:T(8,128)(2,1)S(1)}, bf16[256,128]{1,0:T(8,128)(2,1)S(1)}, u32[]{:S(2)}, u32[]{:S(2)}) collective-permute-start(bf16[256,128]{1,0:T(8,128)(2,1)S(1)} %get-tuple-element.149), channel_id=1, source_target_pairs={{0,2},{2,0},{1,3},{3,1},{4,6},{6,4},{5,7},{7,5},{8,10},{10,8},{9,1... | collective-permute-start | bytes 196616 | tf_op jit(solution)/shard_map/ppermute | solution.py:682
  44.6 1.4 %collective-permute-start.20 = (f32[64,128]{1,0:T(8,128)S(1)}, f32[64,128]{1,0:T(8,128)S(1)}, u32[]{:S(2)}, u32[]{:S(2)}) collective-permute-start(f32[64,128]{1,0:T(8,128)S(1)} %shard_map.135.refs_18_.refs_15_), channel_id=1, source_target_pairs={{0,1},{1,0},{2,3},{3,2},{4,5},{5,4},{6,7},{7,6},{8,9},{9,8},{10,11... | collective-permute-start | bytes 98312 | tf_op jit(solution)/shard_map/ppermute | solution.py:682
